TPU v7x, 256 devices: a whole 4x4x8 slice. The times are simulated.
256 devices in a mesh: ctx: 32 (over y, z), head: 8 (over x, core).
Axes of the slice: x: 4, y: 4, z: 8, core: 2. Of those that a mesh axis runs over, the one named last changes fastest.
Arguments:
- mixer_input: bfloat16 [32768, 8192], P(('ctx', 'head')), may hold values from -0.0625 to 0.0625
- write_vectors: bfloat16 [32768, 1024], P(('ctx', 'head')), may hold values from -0.1875 to 0.1875
- read_vectors: bfloat16 [32768, 1024], P(('ctx', 'head')), may hold values from -0.1875 to 0.1875
- step_sizes: bfloat16 [32768, 128], P(('ctx', 'head')), may hold values from 0.5 to 22937
- fast_rates: float32 [128], replicated, may hold values from 1.5258789e-06 to 0.034
- slow_heads: int32 [64], replicated, may hold values from 0 to 127, as said below
- skip_gains: float32 [128], replicated, may hold values from 0.5 to 1.5
- mixer_grad: bfloat16 [32768, 8192], P(('ctx', 'head')), may hold values from -6 to 6
- queries: bfloat16 [32768, 4096], P(('ctx', 'head')), may hold values from -150 to 150
- attn_keys: bfloat16 [32768, 1024], P(('ctx', 'head')), may hold values from -6 to 6
- attn_values: bfloat16 [32768, 1024], P(('ctx', 'head')), may hold values from -24 to 24
- attn_grad: bfloat16 [32768, 4096], P(('ctx', 'head')), may hold values from -24 to 24
- doc_lengths: int32 [16], replicated, may hold values from 1 to 3072, 32768 in all
Outputs:
- grad_mixer_input: bfloat16 [32768, 8192], P(('ctx', 'head'))
- grad_write: bfloat16 [32768, 1024], P(('ctx', 'head'))
- grad_read: bfloat16 [32768, 1024], P(('ctx', 'head'))
- grad_queries: bfloat16 [32768, 4096], P(('ctx', 'head'))
Inputs may be any that keep to these rules, and one draw needn't show every extreme that they name: `slow_heads`: distinct head numbers.
All inputs are finite; a program needn't handle non-finite values.
Results may differ from a plain program's by a relative error of at most 0.0062.
Values may be sent and summed in bfloat16 or wider, within the bound.
A program may use at most 192 MiB of HBM per device.

v0:
```python
import jax
import jax.numpy as jnp
from jax import lax
from jax.sharding import Mesh
from jax.sharding import PartitionSpec as P

MH = 128
HD = 64
NS = 128
DH = 128
BLOCK = 256
CTX = ("ctx_0", "ctx_1")
CTX_HEAD = ("ctx_0", "ctx_1", "head")
slab_reach = 3


def filled_with(shard, identity):
    return jax.tree.map(
        lambda a, e: jnp.broadcast_to(jnp.asarray(e, a.dtype), a.shape), shard, identity
    )


def entering_2(shard, axes, combine, identity, reverse):
    before = start = filled_with(shard, identity)
    so_far = shard
    for axis in reversed(axes):
        devices, position = (lax.axis_size(axis), lax.axis_index(axis))
        pieces = jax.tree.map(lambda part: lax.all_gather(part, axis), so_far)
        inside, so_far = (start, start)
        for k in reversed(range(devices)) if reverse else range(devices):
            passed = k > position if reverse else k < position
            so_far = combine(so_far, jax.tree.map(lambda part: part[k], pieces))
            inside = jax.tree.map(lambda new, old: jnp.where(passed, new, old), so_far, inside)
        before = combine(inside, before)
    return before


def from_behind(value, axis, steps):
    count = lax.axis_size(axis)
    leading, last = (max(0, -steps), min(count, count - steps))
    return lax.ppermute(value, axis, [(source, source + steps) for source in range(leading, last)])


def doc_index(positions, doc_lengths):
    starts = jnp.cumsum(doc_lengths) - doc_lengths
    match_count = (starts[None, :] <= positions[:, None]).astype(jnp.int32)
    return jnp.sum(match_count, axis=1) - 1


def combine(earlier, latter):
    factor = latter[0]
    return (earlier[0] * factor, factor[..., None, None] * earlier[1] + latter[1])


def stretch_edges(
    stretch_inputs, stretch_write, stretch_read, decay_log, stretch_grads, docs, doc_prev
):
    cumulative = jnp.cumsum(decay_log, axis=1)
    totals = cumulative[:, -1]
    linked = (docs == doc_prev[:, None]).astype(jnp.float32)
    tail_doc = (docs == docs[:, -1:]).astype(jnp.float32)
    stretch_links = jnp.exp(totals) * linked[:, -1][:, None, None]
    entering = jnp.exp(cumulative) * linked[:, :, None, None]
    to_end = jnp.exp(totals[:, None] - cumulative) * tail_doc[:, :, None, None]
    input_weighted = (stretch_inputs.astype(jnp.float32) * to_end[..., None]).astype(jnp.bfloat16)
    grad_weighted = (stretch_grads.astype(jnp.float32) * entering[..., None]).astype(jnp.bfloat16)
    endings = jnp.einsum(
        "ksghp,ksgn->kghpn", input_weighted, stretch_write, preferred_element_type=jnp.float32
    )
    openings = jnp.einsum(
        "ktghp,ktgn->kghpn", grad_weighted, stretch_read, preferred_element_type=jnp.float32
    )
    return (cumulative, stretch_links, to_end, input_weighted, grad_weighted, endings, openings)


def stretch_inner(stretch_inputs, stretch_write, stretch_read, stretch_grads, docs, cumulative):
    block_rows = stretch_inputs.shape[1]
    offsets = jnp.arange(block_rows, dtype=jnp.int32)
    causal = offsets[:, None] >= offsets[None, :]
    same_doc = causal[None] & (docs[:, :, None] == docs[:, None, :])
    cum_heads = jnp.transpose(cumulative, (0, 2, 3, 1))
    log_gaps = cum_heads[..., :, None] - cum_heads[..., None, :]
    decays = jnp.exp(jnp.where(same_doc[:, None, None], log_gaps, -jnp.inf))
    scores = jnp.einsum(
        "ktgn,ksgn->kgts", stretch_read, stretch_write, preferred_element_type=jnp.float32
    )
    mixing = (scores[:, :, None] * decays).astype(jnp.bfloat16)
    input_inner = jnp.einsum(
        "kghts,ktghp->ksghp", mixing, stretch_grads, preferred_element_type=jnp.float32
    )
    inner_products = jnp.einsum(
        "ktghp,ksghp->kghts", stretch_grads, stretch_inputs, preferred_element_type=jnp.float32
    )
    joint_weights = jnp.sum(inner_products * decays, axis=2).astype(jnp.bfloat16)
    read_inner = jnp.einsum(
        "kgts,ksgn->ktgn", joint_weights, stretch_write, preferred_element_type=jnp.float32
    )
    write_inner = jnp.einsum(
        "kgts,ktgn->ksgn", joint_weights, stretch_read, preferred_element_type=jnp.float32
    )
    return (input_inner, write_inner, read_inner)


def mixer_grads(
    inputs_here,
    write_here,
    read_here,
    steps_here,
    grad_here,
    fast_rates,
    slow_heads,
    skip_gains,
    doc_lengths,
    first_row,
    head_index,
    total_rows,
):
    row_count = inputs_here.shape[0]
    local_heads = steps_here.shape[1]
    local_groups = write_here.shape[1] // NS
    per_group = local_heads // local_groups
    stretch_count = row_count // BLOCK
    head_ids = jnp.arange(MH, dtype=jnp.int32)
    slow_mask = jnp.any(head_ids[:, None] == slow_heads[None, :], axis=1)
    rates = jnp.where(slow_mask, 1.0 / total_rows, fast_rates)
    head_start = head_index * local_heads
    rates_here = lax.dynamic_slice_in_dim(rates, head_start, local_heads).reshape(
        local_groups, per_group
    )
    skips_here = lax.dynamic_slice_in_dim(skip_gains, head_start, local_heads).reshape(
        local_groups, per_group
    )
    decay_log = (
        -steps_here.astype(jnp.float32).reshape(stretch_count, BLOCK, local_groups, per_group)
        * rates_here
    )
    shape_x = (stretch_count, BLOCK, local_groups, per_group, HD)
    shape_v = (stretch_count, BLOCK, local_groups, NS)
    stretch_inputs = inputs_here.reshape(shape_x)
    stretch_grads = grad_here.reshape(shape_x)
    stretch_write = write_here.reshape(shape_v)
    stretch_read = read_here.reshape(shape_v)
    positions = first_row + jnp.arange(row_count, dtype=jnp.int32)
    docs = doc_index(positions, doc_lengths).reshape(stretch_count, BLOCK)
    doc_prev = doc_index(
        first_row - 1 + BLOCK * jnp.arange(stretch_count, dtype=jnp.int32), doc_lengths
    )
    cumulative, stretch_links, to_end, input_weighted, grad_weighted, endings, openings = (
        stretch_edges(
            stretch_inputs, stretch_write, stretch_read, decay_log, stretch_grads, docs, doc_prev
        )
    )
    input_inner, write_inner, read_inner = stretch_inner(
        stretch_inputs, stretch_write, stretch_read, stretch_grads, docs, cumulative
    )

    def forward_local(carried, element):
        stretch_link, ending = element
        return (
            (stretch_link[..., None, None] * carried[0] + ending, stretch_link * carried[1]),
            carried,
        )

    def backward_local(carried, element):
        stretch_link, opening = element
        return (
            (opening + stretch_link[..., None, None] * carried[0], stretch_link * carried[1]),
            carried,
        )

    zero_state = jnp.zeros_like(endings[0])
    unit_links = jnp.ones_like(stretch_links[0])
    (device_end, device_link), (local_states, local_links) = lax.scan(
        forward_local, (zero_state, unit_links), (stretch_links, endings)
    )
    (device_open, unused), (local_backs, back_links) = lax.scan(
        backward_local, (zero_state, unit_links), (stretch_links, openings), reverse=True
    )
    state_in = entering_2((device_link, device_end), CTX, combine, (unit_links, zero_state), False)[
        1
    ]
    back_out = entering_2((device_link, device_open), CTX, combine, (unit_links, zero_state), True)[
        1
    ]
    states_low = (local_states + local_links[..., None, None] * state_in).astype(jnp.bfloat16)
    backs_low = (local_backs + back_links[..., None, None] * back_out).astype(jnp.bfloat16)
    read_carried = jnp.einsum(
        "ktghp,kghpn->ktgn", grad_weighted, states_low, preferred_element_type=jnp.float32
    )
    write_carried = jnp.einsum(
        "ksghp,kghpn->ksgn", input_weighted, backs_low, preferred_element_type=jnp.float32
    )
    input_carried = to_end[..., None] * jnp.einsum(
        "ksgn,kghpn->ksghp", stretch_write, backs_low, preferred_element_type=jnp.float32
    )
    grad_input = (
        input_inner + input_carried + skips_here[..., None] * stretch_grads.astype(jnp.float32)
    ).astype(jnp.bfloat16)
    grad_write = (write_inner + write_carried).astype(jnp.bfloat16)
    grad_read = (read_inner + read_carried).astype(jnp.bfloat16)
    return (
        grad_input.reshape(row_count, -1),
        grad_write.reshape(row_count, -1),
        grad_read.reshape(row_count, -1),
    )


def attend_block(
    query_block, grad_block, key_block, value_block, query_pos, key_pos, query_doc, key_doc
):
    scaling = query_block.shape[-1] ** (-0.5)
    logits = (
        jnp.einsum("qrd,kd->rqk", query_block, key_block, preferred_element_type=jnp.float32)
        * scaling
    )
    allowed = (
        (key_pos[None, :] <= query_pos[:, None])
        & (key_pos[None, :] >= 0)
        & (query_doc[:, None] == key_doc[None, :])
    )
    logits = jnp.where(allowed, logits, -jnp.inf)
    row_peaks = jnp.max(logits, axis=-1, keepdims=True)
    weights = jnp.exp(logits - row_peaks)
    probabilities = weights / jnp.sum(weights, axis=-1, keepdims=True)
    grad_probs = jnp.einsum(
        "qrd,kd->rqk", grad_block, value_block, preferred_element_type=jnp.float32
    )
    centre = jnp.sum(probabilities * grad_probs, axis=-1, keepdims=True)
    grad_logits = (probabilities * (grad_probs - centre)).astype(jnp.bfloat16)
    return (
        jnp.einsum("rqk,kd->qrd", grad_logits, key_block, preferred_element_type=jnp.float32)
        * scaling
    )


def attend(
    query_rows, grad_rows, key_rows, value_rows, first_row, lead_rows, doc_reach, doc_lengths
):
    row_count = query_rows.shape[0]
    kv_heads = key_rows.shape[1] // DH
    group_size = query_rows.shape[1] // key_rows.shape[1]
    query_four = query_rows.reshape(row_count, kv_heads, group_size, DH)
    grad_four = grad_rows.reshape(row_count, kv_heads, group_size, DH)
    key_three = key_rows.reshape(-1, kv_heads, DH)
    value_three = value_rows.reshape(-1, kv_heads, DH)
    block_rows = min(128, row_count)
    block_count = row_count // block_rows
    span = doc_reach + block_rows
    query_positions = first_row + jnp.arange(row_count, dtype=jnp.int32)
    key_positions = first_row - lead_rows + jnp.arange(key_rows.shape[0], dtype=jnp.int32)
    query_docs = doc_index(query_positions, doc_lengths)
    key_docs = doc_index(key_positions, doc_lengths)

    def one_item(index):
        block = index // kv_heads
        which = index % kv_heads
        begin = block * block_rows
        key_begin = begin + lead_rows - doc_reach
        query_part = lax.dynamic_index_in_dim(
            lax.dynamic_slice_in_dim(query_four, begin, block_rows, 0), which, 1, keepdims=False
        )
        grad_part = lax.dynamic_index_in_dim(
            lax.dynamic_slice_in_dim(grad_four, begin, block_rows, 0), which, 1, keepdims=False
        )
        key_part = lax.dynamic_index_in_dim(
            lax.dynamic_slice_in_dim(key_three, key_begin, span, 0), which, 1, keepdims=False
        )
        value_part = lax.dynamic_index_in_dim(
            lax.dynamic_slice_in_dim(value_three, key_begin, span, 0), which, 1, keepdims=False
        )
        return attend_block(
            query_part,
            grad_part,
            key_part,
            value_part,
            lax.dynamic_slice_in_dim(query_positions, begin, block_rows, 0),
            lax.dynamic_slice_in_dim(key_positions, key_begin, span, 0),
            lax.dynamic_slice_in_dim(query_docs, begin, block_rows, 0),
            lax.dynamic_slice_in_dim(key_docs, key_begin, span, 0),
        )

    items = lax.map(one_item, jnp.arange(block_count * kv_heads, dtype=jnp.int32))
    items = items.reshape(block_count, kv_heads, block_rows, group_size, DH).transpose(
        0, 2, 1, 3, 4
    )
    return items.reshape(row_count, -1).astype(jnp.bfloat16)


def head_attention(query_rows, key_rows, value_rows, grad_rows, doc_lengths, first_row):
    row_count = query_rows.shape[0]
    earlier_keys = []
    earlier_values = []
    for distance in range(slab_reach, 0, -1):
        fetched = from_behind((key_rows, value_rows), CTX, distance)
        earlier_keys.append(fetched[0])
        earlier_values.append(fetched[1])
    key_all = jnp.concatenate(earlier_keys + [key_rows], axis=0)
    value_all = jnp.concatenate(earlier_values + [value_rows], axis=0)
    lead = slab_reach * row_count
    return attend(query_rows, grad_rows, key_all, value_all, first_row, lead, lead, doc_lengths)


def shards(
    mixer_input,
    write_vectors,
    read_vectors,
    step_sizes,
    fast_rates,
    slow_heads,
    skip_gains,
    mixer_grad,
    queries,
    attn_keys,
    attn_values,
    attn_grad,
    doc_lengths,
):
    head_count = lax.axis_size("head")
    ctx_index = lax.axis_index(CTX)
    head_index = lax.axis_index("head")
    shard_rows = mixer_input.shape[0] * head_count
    total_rows = shard_rows * lax.axis_size(CTX)
    moved = (
        lax.all_to_all(mixer_input, "head", split_axis=1, concat_axis=0, tiled=True),
        lax.all_to_all(write_vectors, "head", split_axis=1, concat_axis=0, tiled=True),
        lax.all_to_all(read_vectors, "head", split_axis=1, concat_axis=0, tiled=True),
        lax.all_to_all(step_sizes, "head", split_axis=1, concat_axis=0, tiled=True),
        lax.all_to_all(mixer_grad, "head", split_axis=1, concat_axis=0, tiled=True),
        lax.all_to_all(queries, "head", split_axis=1, concat_axis=0, tiled=True),
        lax.all_to_all(attn_keys, "head", split_axis=1, concat_axis=0, tiled=True),
        lax.all_to_all(attn_values, "head", split_axis=1, concat_axis=0, tiled=True),
        lax.all_to_all(attn_grad, "head", split_axis=1, concat_axis=0, tiled=True),
    )
    grad_query_heads = head_attention(
        moved[5], moved[6], moved[7], moved[8], doc_lengths, ctx_index * shard_rows
    )
    grad_input, grad_write, grad_read = mixer_grads(
        moved[0],
        moved[1],
        moved[2],
        moved[3],
        moved[4],
        fast_rates,
        slow_heads,
        skip_gains,
        doc_lengths,
        ctx_index * shard_rows,
        head_index,
        total_rows,
    )
    returned = (
        lax.all_to_all(grad_input, "head", split_axis=0, concat_axis=1, tiled=True),
        lax.all_to_all(grad_write, "head", split_axis=0, concat_axis=1, tiled=True),
        lax.all_to_all(grad_read, "head", split_axis=0, concat_axis=1, tiled=True),
        lax.all_to_all(grad_query_heads, "head", split_axis=0, concat_axis=1, tiled=True),
    )
    return (returned[0], returned[1], returned[2], returned[3])


def solution(mesh):
    split = Mesh(mesh.devices.reshape(4, 8, mesh.shape["head"]), ("ctx_0", "ctx_1", "head"))
    return jax.shard_map(
        shards,
        mesh=split,
        in_specs=(
            P(CTX_HEAD, None),
            P(CTX_HEAD, None),
            P(CTX_HEAD, None),
            P(CTX_HEAD, None),
            P(),
            P(),
            P(),
            P(CTX_HEAD, None),
            P(CTX_HEAD, None),
            P(CTX_HEAD, None),
            P(CTX_HEAD, None),
            P(CTX_HEAD, None),
            P(),
        ),
        out_specs=(P(CTX_HEAD, None), P(CTX_HEAD, None), P(CTX_HEAD, None), P(CTX_HEAD, None)),
        check_vma=False,
    )
```

profile of v0, /device:TPU:1, one launch (start us, length us, event | category | flops | bytes accessed | tf_op | source)
XLA Modules:
  0.0 617.0 jit_solution(6818892694384859744)
XLA Ops:
  8.7 6.5 %all-to-all-start.2 = ((bf16[128,8,16]{0,2,1:T(8,128)(2,1)}), bf16[128,8,16]{0,2,1:T(8,128)(2,1)S(1)}, u32[]{:S(2)}, u32[]{:S(2)}) async-start(bf16[128,8,16]{0,2,1:T(8,128)(2,1)} %bitcast.17), calls=%async_computation.2 | async-start | bytes 65536 | tf_op jit(solution)/shard_map/all_to_all | solution.py:327
  32.0 22.2 %all-to-all-done.4 = bf16[128,8,1024]{0,2,1:T(8,128)(2,1)S(1)} async-done(((bf16[128,8,1024]{0,2,1:T(8,128)(2,1)}), bf16[128,8,1024]{0,2,1:T(8,128)(2,1)S(1)}, u32[]{:S(2)}, u32[]{:S(2)}) %all-to-all-start.4) | async-done | bytes 2097184 | tf_op jit(solution)/shard_map/all_to_all | solution.py:324
  70.4 5.2 while.54
  86.3 25.5 %all-to-all-done.3 = bf16[128,8,1024]{0,2,1:T(8,128)(2,1)S(1)} async-done(((bf16[128,8,1024]{0,2,1:T(8,128)(2,1)}), bf16[128,8,1024]{0,2,1:T(8,128)(2,1)S(1)}, u32[]{:S(2)}, u32[]{:S(2)}) %all-to-all-start.3) | async-done | bytes 2097184 | tf_op jit(solution)/shard_map/all_to_all | solution.py:328
  129.3 8.2 %while.53 = (s32[]{:T(128)}, f32[1,16,64,128]{3,2,1,0:T(8,128)S(1)}, f32[1,16]{1,0:T(1,128)S(1)}, f32[4,1,16,64,128]{4,3,2,1,0:T(8,128)}, f32[4,1,16]{2,1,0:T(1,...) while((s32[]{:T(128)}, ...), condition=%wide.region_7.8_spmd.clone, body=%wide.region_6.7_spmd.clone.sunk | while | flops 524340 | bytes 2622994 | solution.py:176
  138.4 14.6 %all-gather.3 = f32[8,1,16]{2,1,0:T(1,128)S(1)} all-gather(f32[1,1,16]{2,1,0:T(1,128)S(1)} %bitcast.562), channel_id=2, replica_groups=mesh['ctx_0'=4,'ctx_1'=8,'head'=8] {'ctx_1'}, dimensions={0}, use_global_device_ids=true | all-gather | bytes 576 | tf_op jit(solution)/shard_map/all_gather | solution.py:28
  159.4 8.6 %all-to-all-start.8 = ((bf16[128,8,128]{2,0,1:T(8,128)(2,1)}), bf16[128,8,128]{2,0,1:T(8,128)(2,1)}, u32[]{:S(2)}, u32[]{:S(2)}) async-start(bf16[128,8,128]{2,0,1:T(8,128)(2,1)} %copy_bitcast_fusion.3), calls=%async_computation.8 | async-start | bytes 524288 | tf_op jit(solution)/shard_map/all_to_all | solution.py:330
  174.6 5.2 all-to-all-start.10
  200.3 5.0 collective-permute-start.1
  207.4 5.0 collective-permute-start.3
  217.9 6.2 %all-to-all-start.11 = ((bf16[128,8,512]{0,2,1:T(8,128)(2,1)}), bf16[128,8,512]{0,2,1:T(8,128)(2,1)}, u32[]{:S(2)}, u32[]{:S(2)}) async-start(bf16[128,8,512]{0,2,1:T(8,128)(2,1)} %bitcast.111), calls=%async_computation.11 | async-start | bytes 2097152 | tf_op jit(solution)/shard_map/all_to_all | solution.py:332
  227.3 6.4 %collective-permute-done.2 = bf16[1024,128]{1,0:T(8,128)(2,1)} collective-permute-done((bf16[1024,128]{1,0:T(8,128)(2,1)}, bf16[1024,128]{1,0:T(8,128)(2,1)}, u32[]{:S(2)}, u32[]{:S(2)}) %collective-permute-start.2) | collective-permute-done | bytes 262176 | tf_op jit(solution)/shard_map/ppermute | solution.py:41
  236.0 13.2 %collective-permute-done.3 = bf16[1024,128]{1,0:T(8,128)(2,1)} collective-permute-done((bf16[1024,128]{1,0:T(8,128)(2,1)}, bf16[1024,128]{1,0:T(8,128)(2,1)}, u32[]{:S(2)}, u32[]{:S(2)}) %collective-permute-start.3) | collective-permute-done | bytes 262176 | tf_op jit(solution)/shard_map/ppermute | solution.py:41
  249.2 7.6 %collective-permute-done.4 = bf16[1024,128]{1,0:T(8,128)(2,1)} collective-permute-done((bf16[1024,128]{1,0:T(8,128)(2,1)}, bf16[1024,128]{1,0:T(8,128)(2,1)}, u32[]{:S(2)}, u32[]{:S(2)}) %collective-permute-start.4) | collective-permute-done | bytes 262176 | tf_op jit(solution)/shard_map/ppermute | solution.py:41
  256.8 10.6 %collective-permute-done.5 = bf16[1024,128]{1,0:T(8,128)(2,1)S(1)} collective-permute-done((bf16[1024,128]{1,0:T(8,128)(2,1)}, bf16[1024,128]{1,0:T(8,128)(2,1)S(1)}, u32[]{:S(2)}, u32[]{:S(2)}) %collective-permute-start.5) | collective-permute-done | bytes 262176 | tf_op jit(solution)/shard_map/ppermute | solution.py:41
  280.3 198.3 %while.52 = (s32[]{:T(128)}, bf16[8,128,4,128]{1,3,2,0:T(8,128)(2,1)}, s32[8]{0:T(128)S(1)}, bf16[4096,1,128]{2,0,1:T(8,128)(2,1)}, s32[4096]{0:T(1024)S(1)}, /*...) while((s32[]{:T(128)}, ...), condition=%wide.region_16.17_spmd, body=%wide.region_12.16_spmd.sunk | while | flops 1702372736 | bytes 31474184 | solution.py:282
  284.7 5.9 fusion.181
  290.6 7.1 %fusion.182 = (f32[4,128]{1,0:T(4,128)S(1)}, f32[3200,128,4]{1,0,2:T(8,128)}) fusion(f32[4,128,3200]{1,2,0:T(8,128)} %get-tuple-element.851, f32[4,128]{1,0:T(4,128)S(1)} %get-tuple-element.852, bf16[1024,1,4,128]{0,3,2,1:T(8,128)(2,1)} %get-tuple-element.968, s32[]{:T(128)S(6)} %select_n.734, bf16[4096,1,128]{2,0,1:T(8,128)(2,1)} %get-tuple-element.967, ...), kind=kOutput, calls=%fused_computation.5.clone.1 | convolution fusion | flops 424345088 | bytes 14061576 | tf_op jit(solution)/shard_map/while/body/eval_jaxpr/qrd,kd->rqk/dot_general | solution.py:225
  297.7 7.6 %fusion.183 = bf16[8,128,4,128]{1,3,2,0:T(8,128)(2,1)} fusion(bf16[8,128,4,128]{1,3,2,0:T(8,128)(2,1)} %get-tuple-element.943, s32[]{:T(128)} %get-tuple-element.942, f32[3200,128,4]{1,0,2:T(8,128)} %get-tuple-element.853, f32[4,128]{1,0:T(4,128)S(1)} %get-tuple-element.854, f32[4,128]{1,0:T(4,128)S(1)} %get-tuple-element.852, ...), kind=kOutput, calls=%fused_computation.16.clone.1 | convolution fusion | flops 850398848 | bytes 9000960 | tf_op jit(solution)/shard_map/while/body/eval_jaxpr/rqk,kd->qrd/dot_general | solution.py:231
  309.7 5.9 fusion.181
  315.6 6.9 %fusion.182 = (f32[4,128]{1,0:T(4,128)S(1)}, f32[3200,128,4]{1,0,2:T(8,128)}) fusion(f32[4,128,3200]{1,2,0:T(8,128)} %get-tuple-element.851, f32[4,128]{1,0:T(4,128)S(1)} %get-tuple-element.852, bf16[1024,1,4,128]{0,3,2,1:T(8,128)(2,1)} %get-tuple-element.968, s32[]{:T(128)S(6)} %select_n.734, bf16[4096,1,128]{2,0,1:T(8,128)(2,1)} %get-tuple-element.967, ...), kind=kOutput, calls=%fused_computation.5.clone.1 | convolution fusion | flops 424345088 | bytes 14061576 | tf_op jit(solution)/shard_map/while/body/eval_jaxpr/qrd,kd->rqk/dot_general | solution.py:225
  322.5 7.5 %fusion.183 = bf16[8,128,4,128]{1,3,2,0:T(8,128)(2,1)} fusion(bf16[8,128,4,128]{1,3,2,0:T(8,128)(2,1)} %get-tuple-element.943, s32[]{:T(128)} %get-tuple-element.942, f32[3200,128,4]{1,0,2:T(8,128)} %get-tuple-element.853, f32[4,128]{1,0:T(4,128)S(1)} %get-tuple-element.854, f32[4,128]{1,0:T(4,128)S(1)} %get-tuple-element.852, ...), kind=kOutput, calls=%fused_computation.16.clone.1 | convolution fusion | flops 850398848 | bytes 9000960 | tf_op jit(solution)/shard_map/while/body/eval_jaxpr/rqk,kd->qrd/dot_general | solution.py:231
  334.4 5.9 fusion.181
  340.3 6.9 %fusion.182 = (f32[4,128]{1,0:T(4,128)S(1)}, f32[3200,128,4]{1,0,2:T(8,128)}) fusion(f32[4,128,3200]{1,2,0:T(8,128)} %get-tuple-element.851, f32[4,128]{1,0:T(4,128)S(1)} %get-tuple-element.852, bf16[1024,1,4,128]{0,3,2,1:T(8,128)(2,1)} %get-tuple-element.968, s32[]{:T(128)S(6)} %select_n.734, bf16[4096,1,128]{2,0,1:T(8,128)(2,1)} %get-tuple-element.967, ...), kind=kOutput, calls=%fused_computation.5.clone.1 | convolution fusion | flops 424345088 | bytes 14061576 | tf_op jit(solution)/shard_map/while/body/eval_jaxpr/qrd,kd->rqk/dot_general | solution.py:225
  347.3 7.5 %fusion.183 = bf16[8,128,4,128]{1,3,2,0:T(8,128)(2,1)} fusion(bf16[8,128,4,128]{1,3,2,0:T(8,128)(2,1)} %get-tuple-element.943, s32[]{:T(128)} %get-tuple-element.942, f32[3200,128,4]{1,0,2:T(8,128)} %get-tuple-element.853, f32[4,128]{1,0:T(4,128)S(1)} %get-tuple-element.854, f32[4,128]{1,0:T(4,128)S(1)} %get-tuple-element.852, ...), kind=kOutput, calls=%fused_computation.16.clone.1 | convolution fusion | flops 850398848 | bytes 9000960 | tf_op jit(solution)/shard_map/while/body/eval_jaxpr/rqk,kd->qrd/dot_general | solution.py:231
  359.2 5.9 fusion.181
  365.1 6.9 %fusion.182 = (f32[4,128]{1,0:T(4,128)S(1)}, f32[3200,128,4]{1,0,2:T(8,128)}) fusion(f32[4,128,3200]{1,2,0:T(8,128)} %get-tuple-element.851, f32[4,128]{1,0:T(4,128)S(1)} %get-tuple-element.852, bf16[1024,1,4,128]{0,3,2,1:T(8,128)(2,1)} %get-tuple-element.968, s32[]{:T(128)S(6)} %select_n.734, bf16[4096,1,128]{2,0,1:T(8,128)(2,1)} %get-tuple-element.967, ...), kind=kOutput, calls=%fused_computation.5.clone.1 | convolution fusion | flops 424345088 | bytes 14061576 | tf_op jit(solution)/shard_map/while/body/eval_jaxpr/qrd,kd->rqk/dot_general | solution.py:225
  372.0 7.5 %fusion.183 = bf16[8,128,4,128]{1,3,2,0:T(8,128)(2,1)} fusion(bf16[8,128,4,128]{1,3,2,0:T(8,128)(2,1)} %get-tuple-element.943, s32[]{:T(128)} %get-tuple-element.942, f32[3200,128,4]{1,0,2:T(8,128)} %get-tuple-element.853, f32[4,128]{1,0:T(4,128)S(1)} %get-tuple-element.854, f32[4,128]{1,0:T(4,128)S(1)} %get-tuple-element.852, ...), kind=kOutput, calls=%fused_computation.16.clone.1 | convolution fusion | flops 850398848 | bytes 9000960 | tf_op jit(solution)/shard_map/while/body/eval_jaxpr/rqk,kd->qrd/dot_general | solution.py:231
  383.9 5.9 fusion.181
  389.8 6.9 %fusion.182 = (f32[4,128]{1,0:T(4,128)S(1)}, f32[3200,128,4]{1,0,2:T(8,128)}) fusion(f32[4,128,3200]{1,2,0:T(8,128)} %get-tuple-element.851, f32[4,128]{1,0:T(4,128)S(1)} %get-tuple-element.852, bf16[1024,1,4,128]{0,3,2,1:T(8,128)(2,1)} %get-tuple-element.968, s32[]{:T(128)S(6)} %select_n.734, bf16[4096,1,128]{2,0,1:T(8,128)(2,1)} %get-tuple-element.967, ...), kind=kOutput, calls=%fused_computation.5.clone.1 | convolution fusion | flops 424345088 | bytes 14061576 | tf_op jit(solution)/shard_map/while/body/eval_jaxpr/qrd,kd->rqk/dot_general | solution.py:225
  396.8 7.5 %fusion.183 = bf16[8,128,4,128]{1,3,2,0:T(8,128)(2,1)} fusion(bf16[8,128,4,128]{1,3,2,0:T(8,128)(2,1)} %get-tuple-element.943, s32[]{:T(128)} %get-tuple-element.942, f32[3200,128,4]{1,0,2:T(8,128)} %get-tuple-element.853, f32[4,128]{1,0:T(4,128)S(1)} %get-tuple-element.854, f32[4,128]{1,0:T(4,128)S(1)} %get-tuple-element.852, ...), kind=kOutput, calls=%fused_computation.16.clone.1 | convolution fusion | flops 850398848 | bytes 9000960 | tf_op jit(solution)/shard_map/while/body/eval_jaxpr/rqk,kd->qrd/dot_general | solution.py:231
  408.7 5.9 fusion.181
  414.6 6.9 %fusion.182 = (f32[4,128]{1,0:T(4,128)S(1)}, f32[3200,128,4]{1,0,2:T(8,128)}) fusion(f32[4,128,3200]{1,2,0:T(8,128)} %get-tuple-element.851, f32[4,128]{1,0:T(4,128)S(1)} %get-tuple-element.852, bf16[1024,1,4,128]{0,3,2,1:T(8,128)(2,1)} %get-tuple-element.968, s32[]{:T(128)S(6)} %select_n.734, bf16[4096,1,128]{2,0,1:T(8,128)(2,1)} %get-tuple-element.967, ...), kind=kOutput, calls=%fused_computation.5.clone.1 | convolution fusion | flops 424345088 | bytes 14061576 | tf_op jit(solution)/shard_map/while/body/eval_jaxpr/qrd,kd->rqk/dot_general | solution.py:225
  421.5 7.5 %fusion.183 = bf16[8,128,4,128]{1,3,2,0:T(8,128)(2,1)} fusion(bf16[8,128,4,128]{1,3,2,0:T(8,128)(2,1)} %get-tuple-element.943, s32[]{:T(128)} %get-tuple-element.942, f32[3200,128,4]{1,0,2:T(8,128)} %get-tuple-element.853, f32[4,128]{1,0:T(4,128)S(1)} %get-tuple-element.854, f32[4,128]{1,0:T(4,128)S(1)} %get-tuple-element.852, ...), kind=kOutput, calls=%fused_computation.16.clone.1 | convolution fusion | flops 850398848 | bytes 9000960 | tf_op jit(solution)/shard_map/while/body/eval_jaxpr/rqk,kd->qrd/dot_general | solution.py:231
  433.4 5.9 fusion.181
  439.3 6.9 %fusion.182 = (f32[4,128]{1,0:T(4,128)S(1)}, f32[3200,128,4]{1,0,2:T(8,128)}) fusion(f32[4,128,3200]{1,2,0:T(8,128)} %get-tuple-element.851, f32[4,128]{1,0:T(4,128)S(1)} %get-tuple-element.852, bf16[1024,1,4,128]{0,3,2,1:T(8,128)(2,1)} %get-tuple-element.968, s32[]{:T(128)S(6)} %select_n.734, bf16[4096,1,128]{2,0,1:T(8,128)(2,1)} %get-tuple-element.967, ...), kind=kOutput, calls=%fused_computation.5.clone.1 | convolution fusion | flops 424345088 | bytes 14061576 | tf_op jit(solution)/shard_map/while/body/eval_jaxpr/qrd,kd->rqk/dot_general | solution.py:225
  446.3 7.5 %fusion.183 = bf16[8,128,4,128]{1,3,2,0:T(8,128)(2,1)} fusion(bf16[8,128,4,128]{1,3,2,0:T(8,128)(2,1)} %get-tuple-element.943, s32[]{:T(128)} %get-tuple-element.942, f32[3200,128,4]{1,0,2:T(8,128)} %get-tuple-element.853, f32[4,128]{1,0:T(4,128)S(1)} %get-tuple-element.854, f32[4,128]{1,0:T(4,128)S(1)} %get-tuple-element.852, ...), kind=kOutput, calls=%fused_computation.16.clone.1 | convolution fusion | flops 850398848 | bytes 9000960 | tf_op jit(solution)/shard_map/while/body/eval_jaxpr/rqk,kd->qrd/dot_general | solution.py:231
  458.2 5.9 fusion.181
  464.1 6.9 %fusion.182 = (f32[4,128]{1,0:T(4,128)S(1)}, f32[3200,128,4]{1,0,2:T(8,128)}) fusion(f32[4,128,3200]{1,2,0:T(8,128)} %get-tuple-element.851, f32[4,128]{1,0:T(4,128)S(1)} %get-tuple-element.852, bf16[1024,1,4,128]{0,3,2,1:T(8,128)(2,1)} %get-tuple-element.968, s32[]{:T(128)S(6)} %select_n.734, bf16[4096,1,128]{2,0,1:T(8,128)(2,1)} %get-tuple-element.967, ...), kind=kOutput, calls=%fused_computation.5.clone.1 | convolution fusion | flops 424345088 | bytes 14061576 | tf_op jit(solution)/shard_map/while/body/eval_jaxpr/qrd,kd->rqk/dot_general | solution.py:225
  471.0 7.5 %fusion.183 = bf16[8,128,4,128]{1,3,2,0:T(8,128)(2,1)} fusion(bf16[8,128,4,128]{1,3,2,0:T(8,128)(2,1)} %get-tuple-element.943, s32[]{:T(128)} %get-tuple-element.942, f32[3200,128,4]{1,0,2:T(8,128)} %get-tuple-element.853, f32[4,128]{1,0:T(4,128)S(1)} %get-tuple-element.854, f32[4,128]{1,0:T(4,128)S(1)} %get-tuple-element.852, ...), kind=kOutput, calls=%fused_computation.16.clone.1 | convolution fusion | flops 850398848 | bytes 9000960 | tf_op jit(solution)/shard_map/while/body/eval_jaxpr/rqk,kd->qrd/dot_general | solution.py:231
  480.8 5.8 all-to-all-start.12
  492.9 5.7 reshape.908
  498.6 11.1 %all_gather.42 = f32[4,1,16]{2,1,0:T(1,128)S(1)} all-gather(f32[1,1,16]{2,1,0:T(1,128)S(1)} %copy-done.31), channel_id=1, replica_groups=mesh['ctx_0'=4,'ctx_1'=8,'head'=8] {'ctx_0'}, dimensions={0}, use_global_device_ids=true | all-gather | bytes 320 | tf_op jit(solution)/shard_map/all_gather | solution.py:28
  509.7 5.2 all_gather.38
  514.9 7.5 %multiply_reduce_fusion = bf16[4,256,256]{2,1,0:T(8,128)(2,1)S(1)} fusion(f32[4,16,256]{2,1,0:T(8,128)S(1)} %copy-done.23, pred[4,256,256]{2,1,0:T(8,128)(4,1)} %compare_and_fusion.1, bf16[4,256,16,64]{1,0,3,2:T(4,128)(2,1)} %reshape.901, bf16[4,256,16,64]{1,0,3,2:T(4,128)(2,1)} %reshape.898), kind=kOutput, calls=%fused_computation.56 | convolution fusion | flops 553385984 | bytes 5046272 | tf_op jit(solution)/shard_map/ktghp,ksghp->kghts/dot_general | solution.py:91
  538.1 8.7 %all-to-all-start.7 = ((bf16[8,128,128]{2,1,0:T(8,128)(2,1)}), bf16[8,128,128]{2,1,0:T(8,128)(2,1)S(1)}, u32[]{:S(2)}, u32[]{:S(2)}) async-start(bf16[8,128,128]{2,1,0:T(8,128)(2,1)} %bitcast.99), calls=%async_computation.7 | async-start | bytes 524288 | tf_op jit(solution)/shard_map/all_to_all | solution.py:354
  558.0 10.0 %fusion.73 = bf16[4,256,1,16,64]{1,4,3,0,2:T(8,128)(2,1)S(1)} fusion(f32[4,16,64,256]{3,2,1,0:T(8,128)} %fusion.134, f32[4,256,1,16,64]{1,0,4,3,2:T(4,128)} %reshape.908, f32[4,16,256]{2,1,0:T(8,128)S(1)} %copy-done.24, f32[4,256,256]{2,1,0:T(8,128)} %fusion.148, pred[4,256,256]{2,1,0:T(8,128)(4,1)S(1)} %copy-done.20, f32[16]{0:T(128)S(1)} %copy-done.34, ...), kind=kOutput, calls=%fused_computation.68 | convolution fusion | flops 558891008 | bytes 14024768 | tf_op jit(solution)/shard_map/kghts,ktghp->ksghp/dot_general | solution.py:88
  586.1 21.0 %all-to-all-done.5 = bf16[8,128,1024]{1,2,0:T(8,128)(2,1)S(1)} async-done(((bf16[8,128,1024]{1,2,0:T(8,128)(2,1)}), bf16[8,128,1024]{1,2,0:T(8,128)(2,1)S(1)}, u32[]{:S(2)}, u32[]{:S(2)}) %all-to-all-start.5) | async-done | bytes 2097184 | tf_op jit(solution)/shard_map/all_to_all | solution.py:352
  (301 shorter events, 221.9 us)
Async XLA Ops:
  7.2 10.1 %copy-start = (bf16[128,1024]{1,0:T(8,128)(2,1)S(1)}, bf16[128,1024]{1,0:T(8,128)(2,1)}, u32[]{:S(2)}) copy-start(bf16[128,1024]{1,0:T(8,128)(2,1)} %param.20) | copy-start | bytes 786436
  8.7 14.2 %all-to-all-start.2 = ((bf16[128,8,16]{0,2,1:T(8,128)(2,1)}), bf16[128,8,16]{0,2,1:T(8,128)(2,1)S(1)}, u32[]{:S(2)}, u32[]{:S(2)}) async-start(bf16[128,8,16]{0,2,1:T(8,128)(2,1)} %bitcast.17), calls=%async_computation.2 | async-start | bytes 65536 | tf_op jit(solution)/shard_map/all_to_all | solution.py:327
  22.9 5.0 copy-start.32
  22.9 31.3 %all-to-all-start.4 = ((bf16[128,8,1024]{0,2,1:T(8,128)(2,1)}), bf16[128,8,1024]{0,2,1:T(8,128)(2,1)S(1)}, u32[]{:S(2)}, u32[]{:S(2)}) async-start(bf16[128,8,1024]{0,2,1:T(8,128)(2,1)} %bitcast.540), calls=%async_computation.4 | async-start | bytes 4194304 | tf_op jit(solution)/shard_map/all_to_all | solution.py:324
  31.2 23.0 %copy-start.18 = (f32[4,16,2,128]{3,2,1,0:T(2,128)}, f32[4,16,2,128]{3,2,1,0:T(2,128)S(1)}, u32[]{:S(2)}) copy-start(f32[4,16,2,128]{3,2,1,0:T(2,128)S(1)} %broadcast.608) | copy-start | bytes 196612
  31.9 22.3 %copy-start.21 = (f32[4,256,1,16]{1,3,2,0:T(8,128)}, f32[4,256,1,16]{1,3,2,0:T(8,128)S(1)}, u32[]{:S(2)}) copy-start(f32[4,256,1,16]{1,3,2,0:T(8,128)S(1)} %copy.332) | copy-start | bytes 196612
  54.2 13.9 %all-to-all-start.1 = ((bf16[128,8,128]{2,0,1:T(8,128)(2,1)}), bf16[128,8,128]{2,0,1:T(8,128)(2,1)S(1)}, u32[]{:S(2)}, u32[]{:S(2)}) async-start(bf16[128,8,128]{2,0,1:T(8,128)(2,1)} %copy_bitcast_fusion.4), calls=%async_computation.1 | async-start | bytes 524288 | tf_op jit(solution)/shard_map/all_to_all | solution.py:325
  58.4 95.8 %all-gather.15.cloned.1.call-start = ((), (), s32[]{:S(2)}) async-start(), calls=%async_computation.16 | async-start | bytes 4718592 | tf_op jit(solution)/shard_map/all_gather | solution.py:28
  75.6 4.9 copy-start.8
  75.6 4.9 copy-start.25
  80.5 5.0 copy-start.19
  80.5 31.3 %all-to-all-start.3 = ((bf16[128,8,1024]{0,2,1:T(8,128)(2,1)}), bf16[128,8,1024]{0,2,1:T(8,128)(2,1)S(1)}, u32[]{:S(2)}, u32[]{:S(2)}) async-start(bf16[128,8,1024]{0,2,1:T(8,128)(2,1)} %bitcast.542), calls=%async_computation.3 | async-start | bytes 4194304 | tf_op jit(solution)/shard_map/all_to_all | solution.py:328
  111.8 6.9 %copy-start.7 = (bf16[128,8,1024]{0,2,1:T(8,128)(2,1)}, bf16[128,8,1024]{0,2,1:T(8,128)(2,1)S(1)}, u32[]{:S(2)}) copy-start(bf16[128,8,1024]{0,2,1:T(8,128)(2,1)S(1)} %all-to-all-done.3) | copy-start | bytes 6291460
  111.8 13.9 %all-to-all-start = ((bf16[128,8,128]{2,0,1:T(8,128)(2,1)}), bf16[128,8,128]{2,0,1:T(8,128)(2,1)S(1)}, u32[]{:S(2)}, u32[]{:S(2)}) async-start(bf16[128,8,128]{2,0,1:T(8,128)(2,1)} %copy_bitcast_fusion.5), calls=%async_computation | async-start | bytes 524288 | tf_op jit(solution)/shard_map/all_to_all | solution.py:326
  116.0 160.7 %all-gather.13.cloned.1.call-start = ((), (), s32[]{:S(2)}) async-start(), calls=%async_computation.15 | async-start | bytes 4718592 | tf_op jit(solution)/shard_map/all_gather | solution.py:28
  138.4 384.1 %all-gather.11.cloned.1.call-start = ((), (), s32[]{:S(2)}) async-start(), calls=%async_computation.14 | async-start | bytes 2621440 | tf_op jit(solution)/shard_map/all_gather | solution.py:28
  157.6 22.3 %copy-start.33 = (f32[128]{0:T(128)S(1)}, f32[128]{0:T(128)}, u32[]{:S(2)}) copy-start(f32[128]{0:T(128)} %param.25) | copy-start | bytes 1540
  157.6 23.0 %copy-start.16 = (bf16[128,4096]{1,0:T(8,128)(2,1)S(1)}, bf16[128,4096]{1,0:T(8,128)(2,1)}, u32[]{:S(2)}) copy-start(bf16[128,4096]{1,0:T(8,128)(2,1)} %param.27) | copy-start | bytes 3145732
  159.4 15.2 %all-to-all-start.8 = ((bf16[128,8,128]{2,0,1:T(8,128)(2,1)}), bf16[128,8,128]{2,0,1:T(8,128)(2,1)}, u32[]{:S(2)}, u32[]{:S(2)}) async-start(bf16[128,8,128]{2,0,1:T(8,128)(2,1)} %copy_bitcast_fusion.3), calls=%async_computation.8 | async-start | bytes 524288 | tf_op jit(solution)/shard_map/all_to_all | solution.py:330
  174.6 11.8 %all-to-all-start.10 = ((bf16[128,8,128]{2,0,1:T(8,128)(2,1)}), bf16[128,8,128]{2,0,1:T(8,128)(2,1)}, u32[]{:S(2)}, u32[]{:S(2)}) async-start(bf16[128,8,128]{2,0,1:T(8,128)(2,1)} %copy_bitcast_fusion.2), calls=%async_computation.10 | async-start | bytes 524288 | tf_op jit(solution)/shard_map/all_to_all | solution.py:331
  186.4 31.5 %all-to-all-start.9 = ((bf16[128,8,512]{0,2,1:T(8,128)(2,1)}), bf16[128,8,512]{0,2,1:T(8,128)(2,1)S(1)}, u32[]{:S(2)}, u32[]{:S(2)}) async-start(bf16[128,8,512]{0,2,1:T(8,128)(2,1)} %bitcast.548), calls=%async_computation.9 | async-start | bytes 2097152 | tf_op jit(solution)/shard_map/all_to_all | solution.py:329
  197.4 26.8 %collective-permute-start = (bf16[1024,128]{1,0:T(8,128)(2,1)}, bf16[1024,128]{1,0:T(8,128)(2,1)}, u32[]{:S(2)}, u32[]{:S(2)}) collective-permute-start(bf16[1024,128]{1,0:T(8,128)(2,1)} %bitcast.102), channel_id=1, source_target_pairs={{0,24},{8,32},{16,40},{24,48},{32,56},{40,64},{48,72},{56,80},{64,... | collective-permute-start | bytes 786440 | tf_op jit(solution)/shard_map/ppermute | solution.py:41
  200.3 27.0 %collective-permute-start.1 = (bf16[1024,128]{1,0:T(8,128)(2,1)}, bf16[1024,128]{1,0:T(8,128)(2,1)}, u32[]{:S(2)}, u32[]{:S(2)}) collective-permute-start(bf16[1024,128]{1,0:T(8,128)(2,1)} %bitcast.102), channel_id=1, source_target_pairs={{0,16},{8,24},{16,32},{24,40},{32,48},{40,56},{48,64},{56,72},{64,... | collective-permute-start | bytes 786440 | tf_op jit(solution)/shard_map/ppermute | solution.py:41
  205.4 28.3 %collective-permute-start.2 = (bf16[1024,128]{1,0:T(8,128)(2,1)}, bf16[1024,128]{1,0:T(8,128)(2,1)}, u32[]{:S(2)}, u32[]{:S(2)}) collective-permute-start(bf16[1024,128]{1,0:T(8,128)(2,1)} %bitcast.102), channel_id=1, source_target_pairs={{0,8},{8,16},{16,24},{24,32},{32,40},{40,48},{48,56},{56,64},{64,7... | collective-permute-start | bytes 786440 | tf_op jit(solution)/shard_map/ppermute | solution.py:41
  207.4 41.8 %collective-permute-start.3 = (bf16[1024,128]{1,0:T(8,128)(2,1)}, bf16[1024,128]{1,0:T(8,128)(2,1)}, u32[]{:S(2)}, u32[]{:S(2)}) collective-permute-start(bf16[1024,128]{1,0:T(8,128)(2,1)} %bitcast.108), channel_id=1, source_target_pairs={{0,24},{8,32},{16,40},{24,48},{32,56},{40,64},{48,72},{56,80},{64,... | collective-permute-start | bytes 786440 | tf_op jit(solution)/shard_map/ppermute | solution.py:41
  212.4 44.4 %collective-permute-start.4 = (bf16[1024,128]{1,0:T(8,128)(2,1)}, bf16[1024,128]{1,0:T(8,128)(2,1)}, u32[]{:S(2)}, u32[]{:S(2)}) collective-permute-start(bf16[1024,128]{1,0:T(8,128)(2,1)} %bitcast.108), channel_id=1, source_target_pairs={{0,16},{8,24},{16,32},{24,40},{32,48},{40,56},{48,64},{56,72},{64,... | collective-permute-start | bytes 786440 | tf_op jit(solution)/shard_map/ppermute | solution.py:41
  217.9 55.6 %all-to-all-start.11 = ((bf16[128,8,512]{0,2,1:T(8,128)(2,1)}), bf16[128,8,512]{0,2,1:T(8,128)(2,1)}, u32[]{:S(2)}, u32[]{:S(2)}) async-start(bf16[128,8,512]{0,2,1:T(8,128)(2,1)} %bitcast.111), calls=%async_computation.11 | async-start | bytes 2097152 | tf_op jit(solution)/shard_map/all_to_all | solution.py:332
  224.1 304.3 %all-gather.9.cloned.1.call-start = ((), (), s32[]{:S(2)}) async-start(), calls=%async_computation.13 | async-start | bytes 2621440 | tf_op jit(solution)/shard_map/all_gather | solution.py:28
  224.1 43.3 %collective-permute-start.5 = (bf16[1024,128]{1,0:T(8,128)(2,1)}, bf16[1024,128]{1,0:T(8,128)(2,1)S(1)}, u32[]{:S(2)}, u32[]{:S(2)}) collective-permute-start(bf16[1024,128]{1,0:T(8,128)(2,1)} %bitcast.108), channel_id=1, source_target_pairs={{0,8},{8,16},{16,24},{24,32},{32,40},{40,48},{48,56},{56,64},{64,7... | collective-permute-start | bytes 786440 | tf_op jit(solution)/shard_map/ppermute | solution.py:41
  480.8 57.3 %all-to-all-start.12 = ((bf16[8,128,512]{2,1,0:T(8,128)(2,1)}), bf16[8,128,512]{2,1,0:T(8,128)(2,1)}, u32[]{:S(2)}, u32[]{:S(2)}) async-start(bf16[8,128,512]{2,1,0:T(8,128)(2,1)} %copy.289), calls=%async_computation.12 | async-start | bytes 2097152 | tf_op jit(solution)/shard_map/all_to_all | solution.py:355
  492.9 5.7 copy-start.31
  492.9 22.0 %copy-start.23 = (f32[4,16,256]{2,1,0:T(8,128)S(1)}, f32[4,16,256]{2,1,0:T(8,128)}, u32[]{:S(2)}) copy-start(f32[4,16,256]{2,1,0:T(8,128)} %reduce_window_sum.41) | copy-start | bytes 196612
  514.9 7.6 %copy-start.11 = (f32[1,1,16,64,128]{4,3,2,1,0:T(8,128)S(1)}, f32[1,1,16,64,128]{4,3,2,1,0:T(8,128)}, u32[]{:S(2)}) copy-start(f32[1,1,16,64,128]{4,3,2,1,0:T(8,128)} %get-tuple-element.672) | copy-start | bytes 1572868
  514.9 7.6 %copy-start.28 = (f32[16]{0:T(128)S(1)}, f32[16]{0:T(128)}, u32[]{:S(2)}) copy-start(f32[16]{0:T(128)} %copy-done.27) | copy-start | bytes 196
  514.9 7.6 %copy-start.29 = (f32[16]{0:T(128)S(1)}, f32[16]{0:T(128)}, u32[]{:S(2)}) copy-start(f32[16]{0:T(128)} %get-tuple-element.682) | copy-start | bytes 196
  522.5 4.0 copy-start.9
  528.4 4.0 copy-start.15
  528.4 5.0 copy-start.5
  528.4 5.0 copy-start.6
  535.3 11.5 %copy-start.14 = (bf16[128,8,128]{2,0,1:T(8,128)(2,1)S(1)}, bf16[128,8,128]{2,0,1:T(8,128)(2,1)}, u32[]{:S(2)}) copy-start(bf16[128,8,128]{2,0,1:T(8,128)(2,1)} %copy-done.13) | copy-start | bytes 786436
  538.1 19.9 %copy-start.10 = (bf16[4,256,16,64]{1,0,3,2:T(4,128)(2,1)S(1)}, bf16[4,256,16,64]{1,0,3,2:T(4,128)(2,1)}, u32[]{:S(2)}) copy-start(bf16[4,256,16,64]{1,0,3,2:T(4,128)(2,1)} %reshape.898) | copy-start | bytes 6291460
  538.1 19.9 %copy-start.20 = (pred[4,256,256]{2,1,0:T(8,128)(4,1)S(1)}, pred[4,256,256]{2,1,0:T(8,128)(4,1)}, u32[]{:S(2)}) copy-start(pred[4,256,256]{2,1,0:T(8,128)(4,1)} %compare_and_fusion.1) | copy-start | bytes 786436
  538.1 19.9 %copy-start.22 = (f32[4,256,1,16]{1,3,2,0:T(8,128)S(1)}, f32[4,256,1,16]{1,3,2,0:T(8,128)}, u32[]{:S(2)}) copy-start(f32[4,256,1,16]{1,3,2,0:T(8,128)} %copy-done.21) | copy-start | bytes 196612
  538.1 19.9 %copy-start.24 = (f32[4,16,256]{2,1,0:T(8,128)S(1)}, f32[4,16,256]{2,1,0:T(8,128)}, u32[]{:S(2)}) copy-start(f32[4,16,256]{2,1,0:T(8,128)} %reduce_window_sum.41) | copy-start | bytes 196612
  538.1 19.9 %copy-start.34 = (f32[16]{0:T(128)S(1)}, f32[16]{0:T(128)}, u32[]{:S(2)}) copy-start(f32[16]{0:T(128)} %dynamic_slice.121) | copy-start | bytes 196
  538.1 15.2 %all-to-all-start.7 = ((bf16[8,128,128]{2,1,0:T(8,128)(2,1)}), bf16[8,128,128]{2,1,0:T(8,128)(2,1)S(1)}, u32[]{:S(2)}, u32[]{:S(2)}) async-start(bf16[8,128,128]{2,1,0:T(8,128)(2,1)} %bitcast.99), calls=%async_computation.7 | async-start | bytes 524288 | tf_op jit(solution)/shard_map/all_to_all | solution.py:354
  553.3 21.9 %all-to-all-start.6 = ((bf16[8,128,128]{2,1,0:T(8,128)(2,1)}), bf16[8,128,128]{2,1,0:T(8,128)(2,1)S(1)}, u32[]{:S(2)}, u32[]{:S(2)}) async-start(bf16[8,128,128]{2,1,0:T(8,128)(2,1)} %bitcast.78), calls=%async_computation.6 | async-start | bytes 524288 | tf_op jit(solution)/shard_map/all_to_all | solution.py:353
  575.9 31.2 %all-to-all-start.5 = ((bf16[8,128,1024]{1,2,0:T(8,128)(2,1)}), bf16[8,128,1024]{1,2,0:T(8,128)(2,1)S(1)}, u32[]{:S(2)}, u32[]{:S(2)}) async-start(bf16[8,128,1024]{1,2,0:T(8,128)(2,1)} %copy.256), calls=%async_computation.5 | async-start | bytes 4194304 | tf_op jit(solution)/shard_map/all_to_all | solution.py:352
  (10 other events, 21.8 us)
Sparse Core Ops, SparseCore 0:
  76.5 56.9 all-gather.14
  138.5 56.9 all-gather.12
  197.3 44.2 all-gather.10
  280.4 34.4 all-gather.8
where the time goes:
time: 628 us; the launch traced here: 617 us
  matrix products  196 us (31%)
  waiting for transfers between devices  118 us (19%)
  starting transfers between devices  94.8 us (15%)
  local copies, waits for them, and re-layouts  84.4 us (13%)
  other arithmetic  72.5 us (12%)
  blocking collectives  30.8 us (5%)
  between operations  14.9 us (2%)
    dot_general x8, matrix products, attend_block(): jnp.einsum('rqk,kd->qrd', grad_logits, key_block, preferred_element_type=...  60 us
    dot_general x8, matrix products, attend_block(): jnp.einsum('qrd,kd->rqk', grad_block, value_block, preferred_element_type...  55.8 us
    sub x8, matrix products, attend_block(): weights = jnp.exp(logits - row_peaks)  47.3 us
    ppermute x6, waiting for transfers between devices, from_behind(): lax.ppermute(value, axis, [(source, source + steps) for source in range(l...  37.8 us
    all_gather x3, blocking collectives, entering_2(): pieces = jax.tree.map(lambda part: lax.all_gather(part, axis), so_far)  30.8 us
    all_to_all x1, waiting for transfers between devices, shards(): lax.all_to_all(mixer_grad, 'head', split_axis=1, concat_axis=0, tiled=True)  25.5 us
    and x8, other arithmetic, attend_block(): (key_pos[None, :] <= query_pos[:, None]) & (key_pos[None, :] >= 0)  22.5 us
    all_to_all x1, waiting for transfers between devices, shards(): lax.all_to_all(mixer_input, 'head', split_axis=1, concat_axis=0, tiled=True)  22.2 us
  transfers between devices with their start and end apart: 23, of which 10 were waited for; matrix products, arithmetic and copies ran while one was open for 55% of the time, Pallas kernels for 0%

commit v1 on v0

--- a/solution.py
+++ b/solution.py
@@ -3,6 +3,7 @@
 from jax import lax
 from jax.sharding import Mesh
 from jax.sharding import PartitionSpec as P
+from jax.lax import all_to_all, axis_size
 
 MH = 128
 HD = 64
@@ -348,10 +349,13 @@
         head_index,
         total_rows,
     )
+    form_point = lambda v0, axis_key: jnp.concatenate(
+        all_to_all(jnp.stack(jnp.split(v0, axis_size(axis_key), 0), 0), axis_key, 0, 0), 1
+    )
     returned = (
         lax.all_to_all(grad_input, "head", split_axis=0, concat_axis=1, tiled=True),
         lax.all_to_all(grad_write, "head", split_axis=0, concat_axis=1, tiled=True),
-        lax.all_to_all(grad_read, "head", split_axis=0, concat_axis=1, tiled=True),
+        form_point(grad_read, axis_key="head"),
         lax.all_to_all(grad_query_heads, "head", split_axis=0, concat_axis=1, tiled=True),
     )
     return (returned[0], returned[1], returned[2], returned[3])

time: 628 us -> 657 us (1.046)
  waiting for transfers between devices: 118 us -> 151 us
    all_gather x4, waiting for transfers between devices: 0.03 us -> 17 us  [entering_2(): pieces = jax.tree.map(lambda part: lax.all_gather(part, axis), so_far)]
    ppermute x6, waiting for transfers between devices: 37.8 us -> 54.4 us  [from_behind(): lax.ppermute(value, axis, [(source, source + steps) for source in range(l...]
    unnamed x78 -> x75, local copies, waits for them, and re-layouts: 19.9 us -> 25.2 us
  transfers between devices with their start and end apart: 23 -> 23, of which waited for: 10 -> 12; matrix products, arithmetic and copies ran while one was open for 55% -> 52% of each run, Pallas kernels for 0% -> 0%
where the time goes in v1:
time: 657 us; the launch traced here: 646 us
  matrix products  194 us (30%)
  waiting for transfers between devices  151 us (23%)
  starting transfers between devices  94.9 us (14%)
  local copies, waits for them, and re-layouts  90.2 us (14%)
  other arithmetic  68.8 us (10%)
  blocking collectives  26.4 us (4%)
  between operations  14.8 us (2%)
    dot_general x8, matrix products, attend_block(): jnp.einsum('rqk,kd->qrd', grad_logits, key_block, preferred_element_type=...  60 us
    dot_general x8, matrix products, attend_block(): jnp.einsum('qrd,kd->rqk', grad_block, value_block, preferred_element_type...  55.6 us
    ppermute x6, waiting for transfers between devices, from_behind(): lax.ppermute(value, axis, [(source, source + steps) for source in range(l...  54.4 us
    sub x8, matrix products, attend_block(): weights = jnp.exp(logits - row_peaks)  47.1 us
    all_gather x3, blocking collectives, entering_2(): pieces = jax.tree.map(lambda part: lax.all_gather(part, axis), so_far)  26.4 us
    ppermute x6, starting transfers between devices, from_behind(): lax.ppermute(value, axis, [(source, source + steps) for source in range(l...  25.7 us
    all_to_all x1, waiting for transfers between devices, shards(): lax.all_to_all(mixer_grad, 'head', split_axis=1, concat_axis=0, tiled=True)  25.5 us
    unnamed x75, local copies, waits for them, and re-layouts  25.2 us
  transfers between devices with their start and end apart: 23, of which 12 were waited for; matrix products, arithmetic and copies ran while one was open for 52% of the time, Pallas kernels for 0%

profile of v1, /device:TPU:1, one launch (start us, length us, event | category | flops | bytes accessed | tf_op | source)
XLA Modules:
  0.0 645.7 jit_solution(9055941103544988271)
XLA Ops:
  8.7 6.5 %all-to-all-start.2 = ((bf16[128,8,16]{0,2,1:T(8,128)(2,1)}), bf16[128,8,16]{0,2,1:T(8,128)(2,1)S(1)}, u32[]{:S(2)}, u32[]{:S(2)}) async-start(bf16[128,8,16]{0,2,1:T(8,128)(2,1)} %bitcast.17), calls=%async_computation.2 | async-start | bytes 65536 | tf_op jit(solution)/shard_map/all_to_all | solution.py:328
  32.0 22.2 %all-to-all-done.4 = bf16[128,8,1024]{0,2,1:T(8,128)(2,1)S(1)} async-done(((bf16[128,8,1024]{0,2,1:T(8,128)(2,1)}), bf16[128,8,1024]{0,2,1:T(8,128)(2,1)S(1)}, u32[]{:S(2)}, u32[]{:S(2)}) %all-to-all-start.4) | async-done | bytes 2097184 | tf_op jit(solution)/shard_map/all_to_all | solution.py:325
  70.3 5.2 while.54
  86.2 25.5 %all-to-all-done.3 = bf16[128,8,1024]{0,2,1:T(8,128)(2,1)S(1)} async-done(((bf16[128,8,1024]{0,2,1:T(8,128)(2,1)}), bf16[128,8,1024]{0,2,1:T(8,128)(2,1)S(1)}, u32[]{:S(2)}, u32[]{:S(2)}) %all-to-all-start.3) | async-done | bytes 2097184 | tf_op jit(solution)/shard_map/all_to_all | solution.py:329
  129.4 8.2 %while.53 = (s32[]{:T(128)}, f32[1,16,64,128]{3,2,1,0:T(8,128)S(1)}, f32[1,16]{1,0:T(1,128)S(1)}, f32[4,1,16,64,128]{4,3,2,1,0:T(8,128)}, f32[4,1,16]{2,1,0:T(1,...) while((s32[]{:T(128)}, ...), condition=%wide.region_7.8_spmd.clone, body=%wide.region_6.7_spmd.clone.sunk | while | flops 524340 | bytes 2622994 | solution.py:177
  162.3 5.4 all-to-all-start.9
  169.6 6.3 collective-permute-start
  175.9 5.9 collective-permute-start.1
  191.7 6.2 all-to-all-start.11
  202.8 10.3 %collective-permute-done.1 = bf16[1024,128]{1,0:T(8,128)(2,1)} collective-permute-done((bf16[1024,128]{1,0:T(8,128)(2,1)S(1)}, bf16[1024,128]{1,0:T(8,128)(2,1)}, u32[]{:S(2)}, u32[]{:S(2)}) %collective-permute-start.1) | collective-permute-done | bytes 262176 | tf_op jit(solution)/shard_map/ppermute | solution.py:42
  213.0 12.5 %collective-permute-done.2 = bf16[1024,128]{1,0:T(8,128)(2,1)} collective-permute-done((bf16[1024,128]{1,0:T(8,128)(2,1)S(1)}, bf16[1024,128]{1,0:T(8,128)(2,1)}, u32[]{:S(2)}, u32[]{:S(2)}) %collective-permute-start.2) | collective-permute-done | bytes 262176 | tf_op jit(solution)/shard_map/ppermute | solution.py:42
  227.7 13.4 %collective-permute-done.3 = bf16[1024,128]{1,0:T(8,128)(2,1)S(1)} collective-permute-done((bf16[1024,128]{1,0:T(8,128)(2,1)S(1)}, bf16[1024,128]{1,0:T(8,128)(2,1)S(1)}, u32[]{:S(2)}, u32[]{:S(2)}) %collective-permute-start.3) | collective-permute-done | bytes 262176 | tf_op jit(solution)/shard_map/ppermute | solution.py:42
  241.2 9.6 %collective-permute-done.4 = bf16[1024,128]{1,0:T(8,128)(2,1)} collective-permute-done((bf16[1024,128]{1,0:T(8,128)(2,1)S(1)}, bf16[1024,128]{1,0:T(8,128)(2,1)}, u32[]{:S(2)}, u32[]{:S(2)}) %collective-permute-start.4) | collective-permute-done | bytes 262176 | tf_op jit(solution)/shard_map/ppermute | solution.py:42
  250.8 8.6 %collective-permute-done.5 = bf16[1024,128]{1,0:T(8,128)(2,1)S(1)} collective-permute-done((bf16[1024,128]{1,0:T(8,128)(2,1)S(1)}, bf16[1024,128]{1,0:T(8,128)(2,1)S(1)}, u32[]{:S(2)}, u32[]{:S(2)}) %collective-permute-start.5) | collective-permute-done | bytes 262176 | tf_op jit(solution)/shard_map/ppermute | solution.py:42
  271.8 13.8 %all-gather.3 = f32[8,1,16]{2,1,0:T(1,128)S(1)} all-gather(f32[1,1,16]{2,1,0:T(1,128)S(1)} %bitcast.610), channel_id=2, replica_groups=mesh['ctx_0'=4,'ctx_1'=8,'head'=8] {'ctx_1'}, dimensions={0}, use_global_device_ids=true | all-gather | bytes 576 | tf_op jit(solution)/shard_map/all_gather | solution.py:29
  289.1 197.8 %while.52 = (s32[]{:T(128)}, bf16[8,128,4,128]{1,3,2,0:T(8,128)(2,1)}, s32[8]{0:T(128)S(1)}, bf16[4096,1,128]{2,0,1:T(8,128)(2,1)}, s32[4096]{0:T(1024)S(1)}, /*...) while((s32[]{:T(128)}, ...), condition=%wide.region_16.17_spmd, body=%wide.region_12.16_spmd.sunk | while | flops 1702372736 | bytes 31474184 | solution.py:283
  293.5 5.9 fusion.189
  299.4 6.9 %fusion.190 = (f32[4,128]{1,0:T(4,128)S(1)}, f32[3200,128,4]{1,0,2:T(8,128)}) fusion(f32[4,128,3200]{1,2,0:T(8,128)} %get-tuple-element.851, f32[4,128]{1,0:T(4,128)S(1)} %get-tuple-element.852, bf16[1024,1,4,128]{0,3,2,1:T(8,128)(2,1)} %get-tuple-element.968, s32[]{:T(128)S(6)} %select_n.734, bf16[4096,1,128]{2,0,1:T(8,128)(2,1)} %get-tuple-element.967, ...), kind=kOutput, calls=%fused_computation.5.clone.1 | convolution fusion | flops 424345088 | bytes 14061576 | tf_op jit(solution)/shard_map/while/body/eval_jaxpr/qrd,kd->rqk/dot_general | solution.py:226
  306.4 7.5 %fusion.191 = bf16[8,128,4,128]{1,3,2,0:T(8,128)(2,1)} fusion(bf16[8,128,4,128]{1,3,2,0:T(8,128)(2,1)} %get-tuple-element.943, s32[]{:T(128)} %get-tuple-element.942, f32[3200,128,4]{1,0,2:T(8,128)} %get-tuple-element.853, f32[4,128]{1,0:T(4,128)S(1)} %get-tuple-element.854, f32[4,128]{1,0:T(4,128)S(1)} %get-tuple-element.852, ...), kind=kOutput, calls=%fused_computation.16.clone.1 | convolution fusion | flops 850398848 | bytes 9000960 | tf_op jit(solution)/shard_map/while/body/eval_jaxpr/rqk,kd->qrd/dot_general | solution.py:232
  318.2 5.9 fusion.189
  324.2 6.9 %fusion.190 = (f32[4,128]{1,0:T(4,128)S(1)}, f32[3200,128,4]{1,0,2:T(8,128)}) fusion(f32[4,128,3200]{1,2,0:T(8,128)} %get-tuple-element.851, f32[4,128]{1,0:T(4,128)S(1)} %get-tuple-element.852, bf16[1024,1,4,128]{0,3,2,1:T(8,128)(2,1)} %get-tuple-element.968, s32[]{:T(128)S(6)} %select_n.734, bf16[4096,1,128]{2,0,1:T(8,128)(2,1)} %get-tuple-element.967, ...), kind=kOutput, calls=%fused_computation.5.clone.1 | convolution fusion | flops 424345088 | bytes 14061576 | tf_op jit(solution)/shard_map/while/body/eval_jaxpr/qrd,kd->rqk/dot_general | solution.py:226
  331.1 7.5 %fusion.191 = bf16[8,128,4,128]{1,3,2,0:T(8,128)(2,1)} fusion(bf16[8,128,4,128]{1,3,2,0:T(8,128)(2,1)} %get-tuple-element.943, s32[]{:T(128)} %get-tuple-element.942, f32[3200,128,4]{1,0,2:T(8,128)} %get-tuple-element.853, f32[4,128]{1,0:T(4,128)S(1)} %get-tuple-element.854, f32[4,128]{1,0:T(4,128)S(1)} %get-tuple-element.852, ...), kind=kOutput, calls=%fused_computation.16.clone.1 | convolution fusion | flops 850398848 | bytes 9000960 | tf_op jit(solution)/shard_map/while/body/eval_jaxpr/rqk,kd->qrd/dot_general | solution.py:232
  343.0 5.9 fusion.189
  348.9 6.9 %fusion.190 = (f32[4,128]{1,0:T(4,128)S(1)}, f32[3200,128,4]{1,0,2:T(8,128)}) fusion(f32[4,128,3200]{1,2,0:T(8,128)} %get-tuple-element.851, f32[4,128]{1,0:T(4,128)S(1)} %get-tuple-element.852, bf16[1024,1,4,128]{0,3,2,1:T(8,128)(2,1)} %get-tuple-element.968, s32[]{:T(128)S(6)} %select_n.734, bf16[4096,1,128]{2,0,1:T(8,128)(2,1)} %get-tuple-element.967, ...), kind=kOutput, calls=%fused_computation.5.clone.1 | convolution fusion | flops 424345088 | bytes 14061576 | tf_op jit(solution)/shard_map/while/body/eval_jaxpr/qrd,kd->rqk/dot_general | solution.py:226
  355.8 7.5 %fusion.191 = bf16[8,128,4,128]{1,3,2,0:T(8,128)(2,1)} fusion(bf16[8,128,4,128]{1,3,2,0:T(8,128)(2,1)} %get-tuple-element.943, s32[]{:T(128)} %get-tuple-element.942, f32[3200,128,4]{1,0,2:T(8,128)} %get-tuple-element.853, f32[4,128]{1,0:T(4,128)S(1)} %get-tuple-element.854, f32[4,128]{1,0:T(4,128)S(1)} %get-tuple-element.852, ...), kind=kOutput, calls=%fused_computation.16.clone.1 | convolution fusion | flops 850398848 | bytes 9000960 | tf_op jit(solution)/shard_map/while/body/eval_jaxpr/rqk,kd->qrd/dot_general | solution.py:232
  367.7 5.9 fusion.189
  373.6 7.0 %fusion.190 = (f32[4,128]{1,0:T(4,128)S(1)}, f32[3200,128,4]{1,0,2:T(8,128)}) fusion(f32[4,128,3200]{1,2,0:T(8,128)} %get-tuple-element.851, f32[4,128]{1,0:T(4,128)S(1)} %get-tuple-element.852, bf16[1024,1,4,128]{0,3,2,1:T(8,128)(2,1)} %get-tuple-element.968, s32[]{:T(128)S(6)} %select_n.734, bf16[4096,1,128]{2,0,1:T(8,128)(2,1)} %get-tuple-element.967, ...), kind=kOutput, calls=%fused_computation.5.clone.1 | convolution fusion | flops 424345088 | bytes 14061576 | tf_op jit(solution)/shard_map/while/body/eval_jaxpr/qrd,kd->rqk/dot_general | solution.py:226
  380.5 7.5 %fusion.191 = bf16[8,128,4,128]{1,3,2,0:T(8,128)(2,1)} fusion(bf16[8,128,4,128]{1,3,2,0:T(8,128)(2,1)} %get-tuple-element.943, s32[]{:T(128)} %get-tuple-element.942, f32[3200,128,4]{1,0,2:T(8,128)} %get-tuple-element.853, f32[4,128]{1,0:T(4,128)S(1)} %get-tuple-element.854, f32[4,128]{1,0:T(4,128)S(1)} %get-tuple-element.852, ...), kind=kOutput, calls=%fused_computation.16.clone.1 | convolution fusion | flops 850398848 | bytes 9000960 | tf_op jit(solution)/shard_map/while/body/eval_jaxpr/rqk,kd->qrd/dot_general | solution.py:232
  392.4 5.9 fusion.189
  398.3 6.9 %fusion.190 = (f32[4,128]{1,0:T(4,128)S(1)}, f32[3200,128,4]{1,0,2:T(8,128)}) fusion(f32[4,128,3200]{1,2,0:T(8,128)} %get-tuple-element.851, f32[4,128]{1,0:T(4,128)S(1)} %get-tuple-element.852, bf16[1024,1,4,128]{0,3,2,1:T(8,128)(2,1)} %get-tuple-element.968, s32[]{:T(128)S(6)} %select_n.734, bf16[4096,1,128]{2,0,1:T(8,128)(2,1)} %get-tuple-element.967, ...), kind=kOutput, calls=%fused_computation.5.clone.1 | convolution fusion | flops 424345088 | bytes 14061576 | tf_op jit(solution)/shard_map/while/body/eval_jaxpr/qrd,kd->rqk/dot_general | solution.py:226
  405.3 7.5 %fusion.191 = bf16[8,128,4,128]{1,3,2,0:T(8,128)(2,1)} fusion(bf16[8,128,4,128]{1,3,2,0:T(8,128)(2,1)} %get-tuple-element.943, s32[]{:T(128)} %get-tuple-element.942, f32[3200,128,4]{1,0,2:T(8,128)} %get-tuple-element.853, f32[4,128]{1,0:T(4,128)S(1)} %get-tuple-element.854, f32[4,128]{1,0:T(4,128)S(1)} %get-tuple-element.852, ...), kind=kOutput, calls=%fused_computation.16.clone.1 | convolution fusion | flops 850398848 | bytes 9000960 | tf_op jit(solution)/shard_map/while/body/eval_jaxpr/rqk,kd->qrd/dot_general | solution.py:232
  417.1 5.9 fusion.189
  423.0 6.9 %fusion.190 = (f32[4,128]{1,0:T(4,128)S(1)}, f32[3200,128,4]{1,0,2:T(8,128)}) fusion(f32[4,128,3200]{1,2,0:T(8,128)} %get-tuple-element.851, f32[4,128]{1,0:T(4,128)S(1)} %get-tuple-element.852, bf16[1024,1,4,128]{0,3,2,1:T(8,128)(2,1)} %get-tuple-element.968, s32[]{:T(128)S(6)} %select_n.734, bf16[4096,1,128]{2,0,1:T(8,128)(2,1)} %get-tuple-element.967, ...), kind=kOutput, calls=%fused_computation.5.clone.1 | convolution fusion | flops 424345088 | bytes 14061576 | tf_op jit(solution)/shard_map/while/body/eval_jaxpr/qrd,kd->rqk/dot_general | solution.py:226
  430.0 7.5 %fusion.191 = bf16[8,128,4,128]{1,3,2,0:T(8,128)(2,1)} fusion(bf16[8,128,4,128]{1,3,2,0:T(8,128)(2,1)} %get-tuple-element.943, s32[]{:T(128)} %get-tuple-element.942, f32[3200,128,4]{1,0,2:T(8,128)} %get-tuple-element.853, f32[4,128]{1,0:T(4,128)S(1)} %get-tuple-element.854, f32[4,128]{1,0:T(4,128)S(1)} %get-tuple-element.852, ...), kind=kOutput, calls=%fused_computation.16.clone.1 | convolution fusion | flops 850398848 | bytes 9000960 | tf_op jit(solution)/shard_map/while/body/eval_jaxpr/rqk,kd->qrd/dot_general | solution.py:232
  441.9 5.9 fusion.189
  447.7 6.9 %fusion.190 = (f32[4,128]{1,0:T(4,128)S(1)}, f32[3200,128,4]{1,0,2:T(8,128)}) fusion(f32[4,128,3200]{1,2,0:T(8,128)} %get-tuple-element.851, f32[4,128]{1,0:T(4,128)S(1)} %get-tuple-element.852, bf16[1024,1,4,128]{0,3,2,1:T(8,128)(2,1)} %get-tuple-element.968, s32[]{:T(128)S(6)} %select_n.734, bf16[4096,1,128]{2,0,1:T(8,128)(2,1)} %get-tuple-element.967, ...), kind=kOutput, calls=%fused_computation.5.clone.1 | convolution fusion | flops 424345088 | bytes 14061576 | tf_op jit(solution)/shard_map/while/body/eval_jaxpr/qrd,kd->rqk/dot_general | solution.py:226
  454.7 7.5 %fusion.191 = bf16[8,128,4,128]{1,3,2,0:T(8,128)(2,1)} fusion(bf16[8,128,4,128]{1,3,2,0:T(8,128)(2,1)} %get-tuple-element.943, s32[]{:T(128)} %get-tuple-element.942, f32[3200,128,4]{1,0,2:T(8,128)} %get-tuple-element.853, f32[4,128]{1,0:T(4,128)S(1)} %get-tuple-element.854, f32[4,128]{1,0:T(4,128)S(1)} %get-tuple-element.852, ...), kind=kOutput, calls=%fused_computation.16.clone.1 | convolution fusion | flops 850398848 | bytes 9000960 | tf_op jit(solution)/shard_map/while/body/eval_jaxpr/rqk,kd->qrd/dot_general | solution.py:232
  466.6 5.9 fusion.189
  472.5 6.9 %fusion.190 = (f32[4,128]{1,0:T(4,128)S(1)}, f32[3200,128,4]{1,0,2:T(8,128)}) fusion(f32[4,128,3200]{1,2,0:T(8,128)} %get-tuple-element.851, f32[4,128]{1,0:T(4,128)S(1)} %get-tuple-element.852, bf16[1024,1,4,128]{0,3,2,1:T(8,128)(2,1)} %get-tuple-element.968, s32[]{:T(128)S(6)} %select_n.734, bf16[4096,1,128]{2,0,1:T(8,128)(2,1)} %get-tuple-element.967, ...), kind=kOutput, calls=%fused_computation.5.clone.1 | convolution fusion | flops 424345088 | bytes 14061576 | tf_op jit(solution)/shard_map/while/body/eval_jaxpr/qrd,kd->rqk/dot_general | solution.py:226
  479.4 7.5 %fusion.191 = bf16[8,128,4,128]{1,3,2,0:T(8,128)(2,1)} fusion(bf16[8,128,4,128]{1,3,2,0:T(8,128)(2,1)} %get-tuple-element.943, s32[]{:T(128)} %get-tuple-element.942, f32[3200,128,4]{1,0,2:T(8,128)} %get-tuple-element.853, f32[4,128]{1,0:T(4,128)S(1)} %get-tuple-element.854, f32[4,128]{1,0:T(4,128)S(1)} %get-tuple-element.852, ...), kind=kOutput, calls=%fused_computation.16.clone.1 | convolution fusion | flops 850398848 | bytes 9000960 | tf_op jit(solution)/shard_map/while/body/eval_jaxpr/rqk,kd->qrd/dot_general | solution.py:232
  489.2 8.9 %all-to-all-start.12 = ((bf16[8,128,512]{2,1,0:T(8,128)(2,1)}), bf16[8,128,512]{2,1,0:T(8,128)(2,1)}, u32[]{:S(2)}, u32[]{:S(2)}) async-start(bf16[8,128,512]{2,1,0:T(8,128)(2,1)} %copy.289), calls=%async_computation.12 | async-start | bytes 2097152 | tf_op jit(solution)/shard_map/all_to_all | solution.py:359
  504.7 5.6 reshape.915
  510.3 7.2 %all_gather.42 = f32[4,1,16]{2,1,0:T(1,128)S(1)} all-gather(f32[1,1,16]{2,1,0:T(1,128)S(1)} %get-tuple-element.685), channel_id=1, replica_groups=mesh['ctx_0'=4,'ctx_1'=8,'head'=8] {'ctx_0'}, dimensions={0}, use_global_device_ids=true | all-gather | bytes 320 | tf_op jit(solution)/shard_map/all_gather | solution.py:29
  517.5 5.3 all_gather.38
  526.4 8.2 %multiply_reduce_fusion = bf16[4,256,256]{2,1,0:T(8,128)(2,1)} fusion(f32[4,16,256]{2,1,0:T(8,128)S(1)} %copy-done.23, pred[4,256,256]{2,1,0:T(8,128)(4,1)S(1)} %copy-done.20, bf16[4,256,16,64]{1,0,3,2:T(4,128)(2,1)} %reshape.905, bf16[4,256,16,64]{1,0,3,2:T(4,128)(2,1)} %reshape.902), kind=kOutput, calls=%fused_computation.56 | convolution fusion | flops 553385984 | bytes 5046272 | tf_op jit(solution)/shard_map/ktghp,ksghp->kghts/dot_general | solution.py:92
  544.4 16.9 %all-gather.9.cloned.1.call-done = f32[4,1,16,64,128]{4,3,2,1,0:T(8,128)} async-done(((f32[1,1,16,64,128]{4,3,2,1,0:T(8,128)}), f32[4,1,16,64,128]{4,3,2,1,0:T(8,128)}) %all-gather.9.cloned.1.call-update) | async-done | bytes 2097168 | tf_op jit(solution)/shard_map/all_gather | solution.py:29
  586.8 10.0 %fusion.73 = bf16[4,256,1,16,64]{1,4,3,0,2:T(8,128)(2,1)S(1)} fusion(f32[4,16,64,256]{3,2,1,0:T(8,128)} %fusion.142, f32[4,256,1,16,64]{1,0,4,3,2:T(4,128)} %reshape.915, f32[4,16,256]{2,1,0:T(8,128)S(1)} %copy-done.24, f32[4,256,256]{2,1,0:T(8,128)} %fusion.156, pred[4,256,256]{2,1,0:T(8,128)(4,1)S(1)} %copy-done.20, f32[16]{0:T(128)S(1)} %copy-done.29, ...), kind=kOutput, calls=%fused_computation.68 | convolution fusion | flops 558891008 | bytes 14024768 | tf_op jit(solution)/shard_map/kghts,ktghp->ksghp/dot_general | solution.py:89
  614.9 20.9 %all-to-all-done.5 = bf16[8,128,1024]{1,2,0:T(8,128)(2,1)S(1)} async-done(((bf16[8,128,1024]{1,2,0:T(8,128)(2,1)}), bf16[8,128,1024]{1,2,0:T(8,128)(2,1)S(1)}, u32[]{:S(2)}, u32[]{:S(2)}) %all-to-all-start.5) | async-done | bytes 2097184 | tf_op jit(solution)/shard_map/all_to_all | solution.py:356
  (299 shorter events, 233.1 us)
Async XLA Ops:
  7.2 10.1 %copy-start = (bf16[128,1024]{1,0:T(8,128)(2,1)S(1)}, bf16[128,1024]{1,0:T(8,128)(2,1)}, u32[]{:S(2)}) copy-start(bf16[128,1024]{1,0:T(8,128)(2,1)} %param.20) | copy-start | bytes 786436
  8.7 14.2 %all-to-all-start.2 = ((bf16[128,8,16]{0,2,1:T(8,128)(2,1)}), bf16[128,8,16]{0,2,1:T(8,128)(2,1)S(1)}, u32[]{:S(2)}, u32[]{:S(2)}) async-start(bf16[128,8,16]{0,2,1:T(8,128)(2,1)} %bitcast.17), calls=%async_computation.2 | async-start | bytes 65536 | tf_op jit(solution)/shard_map/all_to_all | solution.py:328
  22.9 5.0 copy-start.27
  22.9 31.3 %all-to-all-start.4 = ((bf16[128,8,1024]{0,2,1:T(8,128)(2,1)}), bf16[128,8,1024]{0,2,1:T(8,128)(2,1)S(1)}, u32[]{:S(2)}, u32[]{:S(2)}) async-start(bf16[128,8,1024]{0,2,1:T(8,128)(2,1)} %bitcast.572), calls=%async_computation.4 | async-start | bytes 4194304 | tf_op jit(solution)/shard_map/all_to_all | solution.py:325
  31.9 29.2 %copy-start.21 = (f32[4,256,1,16]{1,3,2,0:T(8,128)}, f32[4,256,1,16]{1,3,2,0:T(8,128)S(1)}, u32[]{:S(2)}) copy-start(f32[4,256,1,16]{1,3,2,0:T(8,128)S(1)} %copy.332) | copy-start | bytes 196612
  54.2 13.9 %all-to-all-start.1 = ((bf16[128,8,128]{2,0,1:T(8,128)(2,1)}), bf16[128,8,128]{2,0,1:T(8,128)(2,1)S(1)}, u32[]{:S(2)}, u32[]{:S(2)}) async-start(bf16[128,8,128]{2,0,1:T(8,128)(2,1)} %copy_bitcast_fusion.4), calls=%async_computation.1 | async-start | bytes 524288 | tf_op jit(solution)/shard_map/all_to_all | solution.py:326
  58.4 227.3 %all-gather.15.cloned.1.call-start = ((), (), s32[]{:S(2)}) async-start(), calls=%async_computation.16 | async-start | bytes 4718592 | tf_op jit(solution)/shard_map/all_gather | solution.py:29
  75.5 4.9 copy-start.8
  75.5 4.9 copy-start.25
  80.5 5.0 copy-start.19
  80.5 31.3 %all-to-all-start.3 = ((bf16[128,8,1024]{0,2,1:T(8,128)(2,1)}), bf16[128,8,1024]{0,2,1:T(8,128)(2,1)S(1)}, u32[]{:S(2)}, u32[]{:S(2)}) async-start(bf16[128,8,1024]{0,2,1:T(8,128)(2,1)} %bitcast.574), calls=%async_computation.3 | async-start | bytes 4194304 | tf_op jit(solution)/shard_map/all_to_all | solution.py:329
  111.8 11.3 %copy-start.7 = (bf16[128,8,1024]{0,2,1:T(8,128)(2,1)}, bf16[128,8,1024]{0,2,1:T(8,128)(2,1)S(1)}, u32[]{:S(2)}) copy-start(bf16[128,8,1024]{0,2,1:T(8,128)(2,1)S(1)} %all-to-all-done.3) | copy-start | bytes 6291460
  111.8 13.9 %all-to-all-start = ((bf16[128,8,128]{2,0,1:T(8,128)(2,1)}), bf16[128,8,128]{2,0,1:T(8,128)(2,1)S(1)}, u32[]{:S(2)}, u32[]{:S(2)}) async-start(bf16[128,8,128]{2,0,1:T(8,128)(2,1)} %copy_bitcast_fusion.5), calls=%async_computation | async-start | bytes 524288 | tf_op jit(solution)/shard_map/all_to_all | solution.py:327
  116.0 406.9 %all-gather.13.cloned.1.call-start = ((), (), s32[]{:S(2)}) async-start(), calls=%async_computation.15 | async-start | bytes 4718592 | tf_op jit(solution)/shard_map/all_gather | solution.py:29
  137.6 18.2 %copy-start.28 = (f32[128]{0:T(128)S(1)}, f32[128]{0:T(128)}, u32[]{:S(2)}) copy-start(f32[128]{0:T(128)} %param.25) | copy-start | bytes 1540
  140.1 11.3 %all-to-all-start.8 = ((bf16[128,8,128]{2,0,1:T(8,128)(2,1)}), bf16[128,8,128]{2,0,1:T(8,128)(2,1)S(1)}, u32[]{:S(2)}, u32[]{:S(2)}) async-start(bf16[128,8,128]{2,0,1:T(8,128)(2,1)} %copy_bitcast_fusion.3), calls=%async_computation.8 | async-start | bytes 524288 | tf_op jit(solution)/shard_map/all_to_all | solution.py:331
  151.4 10.9 %all-to-all-start.10 = ((bf16[128,8,128]{2,0,1:T(8,128)(2,1)}), bf16[128,8,128]{2,0,1:T(8,128)(2,1)S(1)}, u32[]{:S(2)}, u32[]{:S(2)}) async-start(bf16[128,8,128]{2,0,1:T(8,128)(2,1)} %copy_bitcast_fusion.2), calls=%async_computation.10 | async-start | bytes 524288 | tf_op jit(solution)/shard_map/all_to_all | solution.py:332
  162.3 29.4 %all-to-all-start.9 = ((bf16[128,8,512]{0,2,1:T(8,128)(2,1)}), bf16[128,8,512]{0,2,1:T(8,128)(2,1)}, u32[]{:S(2)}, u32[]{:S(2)}) async-start(bf16[128,8,512]{0,2,1:T(8,128)(2,1)} %bitcast.580), calls=%async_computation.9 | async-start | bytes 2097152 | tf_op jit(solution)/shard_map/all_to_all | solution.py:330
  169.6 28.4 %collective-permute-start = (bf16[1024,128]{1,0:T(8,128)(2,1)S(1)}, bf16[1024,128]{1,0:T(8,128)(2,1)}, u32[]{:S(2)}, u32[]{:S(2)}) collective-permute-start(bf16[1024,128]{1,0:T(8,128)(2,1)S(1)} %bitcast.598), channel_id=1, source_target_pairs={{0,24},{8,32},{16,40},{24,48},{32,56},{40,64},{48,72},{56,80},{64,... | collective-permute-start | bytes 786440 | tf_op jit(solution)/shard_map/ppermute | solution.py:42
  175.9 37.1 %collective-permute-start.1 = (bf16[1024,128]{1,0:T(8,128)(2,1)S(1)}, bf16[1024,128]{1,0:T(8,128)(2,1)}, u32[]{:S(2)}, u32[]{:S(2)}) collective-permute-start(bf16[1024,128]{1,0:T(8,128)(2,1)S(1)} %bitcast.599), channel_id=1, source_target_pairs={{0,16},{8,24},{16,32},{24,40},{32,48},{40,56},{48,64},{56,72},{64,... | collective-permute-start | bytes 786440 | tf_op jit(solution)/shard_map/ppermute | solution.py:42
  181.7 43.8 %collective-permute-start.2 = (bf16[1024,128]{1,0:T(8,128)(2,1)S(1)}, bf16[1024,128]{1,0:T(8,128)(2,1)}, u32[]{:S(2)}, u32[]{:S(2)}) collective-permute-start(bf16[1024,128]{1,0:T(8,128)(2,1)S(1)} %bitcast.600), channel_id=1, source_target_pairs={{0,8},{8,16},{16,24},{24,32},{32,40},{40,48},{48,56},{56,64},{64,7... | collective-permute-start | bytes 786440 | tf_op jit(solution)/shard_map/ppermute | solution.py:42
  184.4 56.8 %collective-permute-start.3 = (bf16[1024,128]{1,0:T(8,128)(2,1)S(1)}, bf16[1024,128]{1,0:T(8,128)(2,1)S(1)}, u32[]{:S(2)}, u32[]{:S(2)}) collective-permute-start(bf16[1024,128]{1,0:T(8,128)(2,1)S(1)} %bitcast.594), channel_id=1, source_target_pairs={{0,24},{8,32},{16,40},{24,48},{32,56},{40,64},{48,72},{56,80},{64,... | collective-permute-start | bytes 786440 | tf_op jit(solution)/shard_map/ppermute | solution.py:42
  185.7 65.0 %collective-permute-start.4 = (bf16[1024,128]{1,0:T(8,128)(2,1)S(1)}, bf16[1024,128]{1,0:T(8,128)(2,1)}, u32[]{:S(2)}, u32[]{:S(2)}) collective-permute-start(bf16[1024,128]{1,0:T(8,128)(2,1)S(1)} %bitcast.595), channel_id=1, source_target_pairs={{0,16},{8,24},{16,32},{24,40},{32,48},{40,56},{48,64},{56,72},{64,... | collective-permute-start | bytes 786440 | tf_op jit(solution)/shard_map/ppermute | solution.py:42
  191.7 74.9 %all-to-all-start.11 = ((bf16[128,8,512]{0,2,1:T(8,128)(2,1)}), bf16[128,8,512]{0,2,1:T(8,128)(2,1)}, u32[]{:S(2)}, u32[]{:S(2)}) async-start(bf16[128,8,512]{0,2,1:T(8,128)(2,1)} %bitcast.579), calls=%async_computation.11 | async-start | bytes 2097152 | tf_op jit(solution)/shard_map/all_to_all | solution.py:333
  198.0 336.7 %all-gather.11.cloned.1.call-start = ((), (), s32[]{:S(2)}) async-start(), calls=%async_computation.14 | async-start | bytes 2621440 | tf_op jit(solution)/shard_map/all_gather | solution.py:29
  198.0 61.4 %collective-permute-start.5 = (bf16[1024,128]{1,0:T(8,128)(2,1)S(1)}, bf16[1024,128]{1,0:T(8,128)(2,1)S(1)}, u32[]{:S(2)}, u32[]{:S(2)}) collective-permute-start(bf16[1024,128]{1,0:T(8,128)(2,1)S(1)} %bitcast.596), channel_id=1, source_target_pairs={{0,8},{8,16},{16,24},{24,32},{32,40},{40,48},{48,56},{56,64},{64,7... | collective-permute-start | bytes 786440 | tf_op jit(solution)/shard_map/ppermute | solution.py:42
  489.2 81.3 %all-to-all-start.12 = ((bf16[8,128,512]{2,1,0:T(8,128)(2,1)}), bf16[8,128,512]{2,1,0:T(8,128)(2,1)}, u32[]{:S(2)}, u32[]{:S(2)}) async-start(bf16[8,128,512]{2,1,0:T(8,128)(2,1)} %copy.289), calls=%async_computation.12 | async-start | bytes 2097152 | tf_op jit(solution)/shard_map/all_to_all | solution.py:359
  498.1 63.2 %all-gather.9.cloned.1.call-start = ((), (), s32[]{:S(2)}) async-start(), calls=%async_computation.13 | async-start | bytes 2621440 | tf_op jit(solution)/shard_map/all_gather | solution.py:29
  522.9 3.5 copy-start.20
  522.9 3.5 copy-start.23
  526.4 8.2 %copy-start.11 = (f32[1,1,16,64,128]{4,3,2,1,0:T(8,128)S(1)}, f32[1,1,16,64,128]{4,3,2,1,0:T(8,128)}, u32[]{:S(2)}) copy-start(f32[1,1,16,64,128]{4,3,2,1,0:T(8,128)} %get-tuple-element.672) | copy-start | bytes 1572868
  534.7 4.0 copy-start.9
  534.7 4.0 copy-start.26
  539.8 21.6 %copy-start.12 = (f32[1,1,16,64,128]{4,3,2,1,0:T(8,128)S(1)}, f32[1,1,16,64,128]{4,3,2,1,0:T(8,128)}, u32[]{:S(2)}) copy-start(f32[1,1,16,64,128]{4,3,2,1,0:T(8,128)} %get-tuple-element.674) | copy-start | bytes 1572868
  539.8 21.6 %copy-start.15 = (f32[1,1,16,64,128]{4,3,2,1,0:T(8,128)S(1)}, f32[1,1,16,64,128]{4,3,2,1,0:T(8,128)}, u32[]{:S(2)}) copy-start(f32[1,1,16,64,128]{4,3,2,1,0:T(8,128)} %get-tuple-element.675) | copy-start | bytes 1572868
  561.4 4.5 copy-start.5
  561.4 4.5 copy-start.6
  567.7 7.9 %copy-start.14 = (bf16[4,256,256]{2,1,0:T(8,128)(2,1)S(1)}, bf16[4,256,256]{2,1,0:T(8,128)(2,1)}, u32[]{:S(2)}) copy-start(bf16[4,256,256]{2,1,0:T(8,128)(2,1)} %multiply_reduce_fusion) | copy-start | bytes 1572868
  570.5 16.2 %copy-start.10 = (bf16[4,256,16,64]{1,0,3,2:T(4,128)(2,1)S(1)}, bf16[4,256,16,64]{1,0,3,2:T(4,128)(2,1)}, u32[]{:S(2)}) copy-start(bf16[4,256,16,64]{1,0,3,2:T(4,128)(2,1)} %reshape.902) | copy-start | bytes 6291460
  570.5 16.2 %copy-start.22 = (f32[4,256,1,16]{1,3,2,0:T(8,128)S(1)}, f32[4,256,1,16]{1,3,2,0:T(8,128)}, u32[]{:S(2)}) copy-start(f32[4,256,1,16]{1,3,2,0:T(8,128)} %copy-done.21) | copy-start | bytes 196612
  570.5 16.3 %copy-start.24 = (f32[4,16,256]{2,1,0:T(8,128)S(1)}, f32[4,16,256]{2,1,0:T(8,128)}, u32[]{:S(2)}) copy-start(f32[4,16,256]{2,1,0:T(8,128)} %reduce_window_sum.41) | copy-start | bytes 196612
  570.5 16.3 %copy-start.29 = (f32[16]{0:T(128)S(1)}, f32[16]{0:T(128)}, u32[]{:S(2)}) copy-start(f32[16]{0:T(128)} %dynamic_slice.121) | copy-start | bytes 196
  570.5 11.6 %all-to-all-start.7 = ((bf16[8,128,128]{2,1,0:T(8,128)(2,1)}), bf16[8,128,128]{2,1,0:T(8,128)(2,1)S(1)}, u32[]{:S(2)}, u32[]{:S(2)}) async-start(bf16[8,128,128]{2,1,0:T(8,128)(2,1)} %fusion.132), calls=%async_computation.7 | async-start | bytes 524288 | tf_op jit(solution)/shard_map/all_to_all | solution.py:353
  582.1 14.7 %copy-start.16 = (bf16[8,128,128]{2,1,0:T(8,128)(2,1)}, bf16[8,128,128]{2,1,0:T(8,128)(2,1)S(1)}, u32[]{:S(2)}) copy-start(bf16[8,128,128]{2,1,0:T(8,128)(2,1)S(1)} %all-to-all-done.7) | copy-start | bytes 786436
  582.1 21.9 %all-to-all-start.6 = ((bf16[8,128,128]{2,1,0:T(8,128)(2,1)}), bf16[8,128,128]{2,1,0:T(8,128)(2,1)S(1)}, u32[]{:S(2)}, u32[]{:S(2)}) async-start(bf16[8,128,128]{2,1,0:T(8,128)(2,1)} %bitcast.78), calls=%async_computation.6 | async-start | bytes 524288 | tf_op jit(solution)/shard_map/all_to_all | solution.py:357
  604.7 31.2 %all-to-all-start.5 = ((bf16[8,128,1024]{1,2,0:T(8,128)(2,1)}), bf16[8,128,1024]{1,2,0:T(8,128)(2,1)S(1)}, u32[]{:S(2)}, u32[]{:S(2)}) async-start(bf16[8,128,1024]{1,2,0:T(8,128)(2,1)} %copy.256), calls=%async_computation.5 | async-start | bytes 4194304 | tf_op jit(solution)/shard_map/all_to_all | solution.py:356
  609.5 3.0 copy-start.17
  635.8 2.9 copy-start.1
  (5 other events, 5.5 us)
Sparse Core Ops, SparseCore 0:
  76.5 56.9 all-gather.14
  138.5 90.3 all-gather.12
  289.3 35.6 all-gather.10
  526.5 34.7 all-gather.8
